TPU v7x, 128 devices: a whole 4x4x4 slice. The times are simulated.
128 devices in a mesh: rows: 128 (over x, y, z, core).
Axes of the slice: x: 4, y: 4, z: 4, core: 2. Of those that a mesh axis runs over, the one named last changes fastest.
Arguments:
- source: float32 [512, 2048], P('rows'), may hold values from -60 to 60
- observed: float32 [512, 2048], P('rows'), may hold values from -4 to 4
- precision: float32 [512, 2048], P('rows'), may hold values from 1 to 10
- conductivity: float32 [512, 2048], P('rows'), may hold values from 0.5 to 2
- log_field: float32 [16, 512, 2048], P(None, 'rows'), may hold values from -4 to 4
- noise_field: float32 [16, 512, 2048], P(None, 'rows'), may hold values from -6 to 6
- subspace_noise: float32 [16, 256], replicated, may hold values from -6 to 6
- eigenvalues: float32 [256], replicated, may hold values from 0.1 to 100
- basis: bfloat16 [256, 512, 2048], P(None, 'rows'), may hold values from -0.0234375 to 0.0234375
Outputs:
- proposal: float32 [16, 512, 2048], P(None, 'rows')
- new_coef: float32 [16, 256], replicated
All inputs are finite; a program needn't handle non-finite values.
Results may differ from a plain program's by a relative error of at most 0.0003.
The roundings to bfloat16 on the way count: a program that leaves them out, or rounds other values in their place, can miss the bound.
Values sent between devices are 32-bit elements; how exact they have to be, the bound alone decides.
A program may use at most 64 MiB of HBM per device.

v0:
```python
import functools

import jax
import jax.numpy as jnp
from jax import lax
from jax.sharding import Mesh
from jax.sharding import PartitionSpec as P

ITERS = 4
ROWS = ("rows_0", "rows_1", "rows_2", "rows_3")


def extended(value, sides, width):
    for axis, dim in sides:
        count, length = (lax.axis_size(axis), value.shape[dim])
        up = [(i, (i + 1) % count) for i in range(count - 1)]
        down = [(j, i) for i, j in up]
        last = lax.slice_in_dim(value, length - width, length, axis=dim)
        leading = lax.slice_in_dim(value, 0, width, axis=dim)
        before = lax.ppermute(last, axis, up)
        after = lax.ppermute(leading, axis, down)
        value = jnp.concatenate([before, value, after], axis=dim)
    return value


def one_axis_at_a_time(value, axes):
    return functools.reduce(lax.psum, axes, value)


def apply_operator(field, weights, diagonal):
    padded = extended(field, ((ROWS, 1),), 1)
    padded = jnp.pad(padded, ((0, 0), (0, 0), (1, 1)))
    beside_all = weights[0] * padded[:, :-2, 1:-1] + weights[1] * padded[:, 2:, 1:-1]
    beside_all = beside_all + weights[2] * padded[:, 1:-1, :-2] + weights[3] * padded[:, 1:-1, 2:]
    return diagonal * field - beside_all


def chain_dot(left, right):
    return jnp.sum(left * right, axis=(1, 2))


def broadcast_chain(values):
    return values[:, None, None]


def solve_paired(right_side, scaled, applied, current, curvature, weights, diagonal):
    step_length = current / curvature
    direction = scaled
    direction_image = applied
    solution = broadcast_chain(step_length) * direction
    residual = right_side - broadcast_chain(step_length) * direction_image
    for iteration in range(1, ITERS):
        scaled = residual / diagonal
        applied = apply_operator(scaled, weights, diagonal)
        following, curvature = (
            one_axis_at_a_time(chain_dot(residual, scaled), ROWS),
            one_axis_at_a_time(chain_dot(scaled, applied), ROWS),
        )
        factor = following / current
        step_length = following / (curvature - factor * following / step_length)
        direction = scaled + broadcast_chain(factor) * direction
        direction_image = applied + broadcast_chain(factor) * direction_image
        solution = solution + broadcast_chain(step_length) * direction
        residual = residual - broadcast_chain(step_length) * direction_image
        current = following
    return solution


def project(fields, basis):
    return jnp.einsum(
        "cxy,rxy->cr", fields.astype(jnp.bfloat16), basis, preferred_element_type=jnp.float32
    )


def per_device(
    source,
    observed,
    precision,
    conductivity,
    log_field,
    noise_field,
    subspace_noise,
    eigenvalues,
    basis,
):
    position = lax.axis_index(ROWS)
    devices = lax.axis_size(ROWS)
    cond_rows = extended(conductivity, ((ROWS, 0),), 1)
    upper_row = jnp.where(position == 0, conductivity[:1], cond_rows[:1])
    lower_row = jnp.where(position == devices - 1, conductivity[-1:], cond_rows[-1:])
    padded = jnp.concatenate([upper_row, conductivity, lower_row], 0)
    padded = jnp.pad(padded, ((0, 0), (1, 1)), mode="edge")
    weights = (
        0.5 * (conductivity + padded[:-2, 1:-1]),
        0.5 * (conductivity + padded[2:, 1:-1]),
        0.5 * (conductivity + padded[1:-1, :-2]),
        0.5 * (conductivity + padded[1:-1, 2:]),
    )
    reaction = jnp.exp(log_field)
    diagonal = weights[0] + weights[1] + weights[2] + weights[3] + reaction
    forward_side = jnp.broadcast_to(source, log_field.shape)
    scaled = forward_side / diagonal
    applied = apply_operator(scaled, weights, diagonal)
    current, curvature = (
        one_axis_at_a_time(chain_dot(forward_side, scaled), ROWS),
        one_axis_at_a_time(chain_dot(scaled, applied), ROWS),
    )
    state = solve_paired(forward_side, scaled, applied, current, curvature, weights, diagonal)
    adjoint_side = precision * (state - observed)
    scaled = adjoint_side / diagonal
    applied = apply_operator(scaled, weights, diagonal)
    current, curvature = (
        one_axis_at_a_time(chain_dot(adjoint_side, scaled), ROWS),
        one_axis_at_a_time(chain_dot(scaled, applied), ROWS),
    )
    adjoint = solve_paired(adjoint_side, scaled, applied, current, curvature, weights, diagonal)
    gradient = -reaction * adjoint * state
    chains = log_field.shape[0]
    stacked = jnp.concatenate([log_field, noise_field, gradient], 0)
    coefs = one_axis_at_a_time(project(stacked, basis), ROWS)
    state_coef = coefs[:chains]
    noise_coef = coefs[chains : 2 * chains]
    grad_coef = coefs[2 * chains :]
    variance = 1.0 / (1.0 + eigenvalues)
    keep_factor = (2.0 - 0.8 * variance) / (2.0 + 0.8 * variance)
    drift_factor = 1.6 * variance / (2.0 + 0.8 * variance)
    noise_factor = jnp.sqrt(6.4 * variance) / (2.0 + 0.8 * variance)
    new_coef = keep_factor * state_coef - drift_factor * grad_coef + noise_factor * subspace_noise
    correction = (new_coef - 0.6 * state_coef - 0.8 * noise_coef).astype(jnp.bfloat16)
    rebuilt = jnp.einsum("cr,rxy->cxy", correction, basis, preferred_element_type=jnp.float32)
    proposal = 0.6 * log_field + 0.8 * noise_field + rebuilt
    return (proposal, new_coef)


def solution(mesh):
    finer = Mesh(mesh.devices.reshape(4, 4, 4, 2), ("rows_0", "rows_1", "rows_2", "rows_3"))
    return jax.shard_map(
        per_device,
        mesh=finer,
        in_specs=(
            P(ROWS, None),
            P(ROWS, None),
            P(ROWS, None),
            P(ROWS, None),
            P(None, ROWS, None),
            P(None, ROWS, None),
            P(),
            P(),
            P(None, ROWS, None),
        ),
        out_specs=(P(None, ROWS, None), P()),
        check_vma=False,
    )
```

profile of v0, /device:TPU:1, one launch (start us, length us, event | category | flops | bytes accessed | tf_op | source)
XLA Modules:
  0.0 420.1 jit_solution(18267660677121351661)
XLA Ops:
  1.5 4.9 %collective-permute-start = (f32[1,2048]{1,0:T(1,128)S(1)}, f32[1,2048]{1,0:T(1,128)S(1)}, u32[]{:S(2)}, u32[]{:S(2)}) collective-permute-start(f32[1,2048]{1,0:T(1,128)S(1)} %slice.220), channel_id=1, source_target_pairs={{0,1},{1,2},{2,3},{3,4},{4,5},{5,6},{6,7},{7,8},{8,9},{9,10},{10,1... | collective-permute-start | bytes 24584 | tf_op jit(solution)/shard_map/ppermute | solution.py:20
  8.0 1.9 collective-permute-start.1
  9.9 3.6 collective-permute-done.1
  16.9 1.9 collective-permute-start.2
  18.8 2.4 collective-permute-start.3
  21.2 4.1 collective-permute-done.3
  27.4 10.6 %all-reduce.31 = (f32[16]{0:T(128)S(1)}, f32[16]{0:T(128)S(1)}) all-reduce(f32[16]{0:T(128)S(1)} %get-tuple-element.19, f32[16]{0:T(128)S(1)} %get-tuple-element.18), channel_id=1, replica_groups=mesh['rows_0'=4,'rows_1'=4,'rows_2'=4,'rows_3'=2] {'rows_0'}, use_global_device_ids=true, to_apply=%region_1.2 | all-reduce | flops 32 | bytes 256 | tf_op jit(solution)/shard_map/psum | solution.py:27
  38.0 6.7 %all-reduce.23 = (f32[16]{0:T(128)S(1)}, f32[16]{0:T(128)S(1)}) all-reduce(f32[16]{0:T(128)S(1)} %get-tuple-element.66, f32[16]{0:T(128)S(1)} %get-tuple-element.67), channel_id=1, replica_groups=mesh['rows_0'=4,'rows_1'=4,'rows_2'=4,'rows_3'=2] {'rows_1'}, use_global_device_ids=true, to_apply=%region_2.3 | all-reduce | flops 32 | bytes 256 | tf_op jit(solution)/shard_map/psum | solution.py:27
  44.7 14.4 %all-reduce.15 = (f32[16]{0:T(128)S(1)}, f32[16]{0:T(128)S(1)}) all-reduce(f32[16]{0:T(128)S(1)} %get-tuple-element.50, f32[16]{0:T(128)S(1)} %get-tuple-element.51), channel_id=1, replica_groups=mesh['rows_0'=4,'rows_1'=4,'rows_2'=4,'rows_3'=2] {'rows_2'}, use_global_device_ids=true, to_apply=%region_3.4 | all-reduce | flops 32 | bytes 256 | tf_op jit(solution)/shard_map/psum | solution.py:27
  59.1 3.2 all-reduce.39
  62.6 3.9 collective-permute-start.4
  66.5 1.9 collective-permute-start.5
  68.5 4.3 %collective-permute-done.5 = f32[16,1,2048]{2,0,1:T(8,128)S(1)} collective-permute-done((f32[16,1,2048]{2,0,1:T(8,128)S(1)}, f32[16,1,2048]{2,0,1:T(8,128)S(1)}, u32[]{:S(2)}, u32[]{:S(2)}) %collective-permute-start.5) | collective-permute-done | bytes 131104 | tf_op jit(solution)/shard_map/ppermute | solution.py:21
  73.8 6.0 %all-reduce.30 = (f32[16]{0:T(128)S(1)}, f32[16]{0:T(128)S(1)}) all-reduce(f32[16]{0:T(128)S(1)} %get-tuple-element.17, f32[16]{0:T(128)S(1)} %get-tuple-element.16), channel_id=1, replica_groups=mesh['rows_0'=4,'rows_1'=4,'rows_2'=4,'rows_3'=2] {'rows_0'}, use_global_device_ids=true, to_apply=%region_11.12 | all-reduce | flops 32 | bytes 256 | tf_op jit(solution)/shard_map/psum | solution.py:27
  79.8 7.8 %all-reduce.22 = (f32[16]{0:T(128)S(1)}, f32[16]{0:T(128)S(1)}) all-reduce(f32[16]{0:T(128)S(1)} %get-tuple-element.64, f32[16]{0:T(128)S(1)} %get-tuple-element.65), channel_id=1, replica_groups=mesh['rows_0'=4,'rows_1'=4,'rows_2'=4,'rows_3'=2] {'rows_1'}, use_global_device_ids=true, to_apply=%region_12.13 | all-reduce | flops 32 | bytes 256 | tf_op jit(solution)/shard_map/psum | solution.py:27
  87.6 11.7 %all-reduce.14 = (f32[16]{0:T(128)S(1)}, f32[16]{0:T(128)S(1)}) all-reduce(f32[16]{0:T(128)S(1)} %get-tuple-element.48, f32[16]{0:T(128)S(1)} %get-tuple-element.49), channel_id=1, replica_groups=mesh['rows_0'=4,'rows_1'=4,'rows_2'=4,'rows_3'=2] {'rows_2'}, use_global_device_ids=true, to_apply=%region_13.14 | all-reduce | flops 32 | bytes 256 | tf_op jit(solution)/shard_map/psum | solution.py:27
  99.3 2.5 all-reduce.38
  102.2 3.9 collective-permute-start.6
  106.1 1.9 collective-permute-start.7
  108.1 4.3 %collective-permute-done.7 = f32[16,1,2048]{2,0,1:T(8,128)S(1)} collective-permute-done((f32[16,1,2048]{2,0,1:T(8,128)S(1)}, f32[16,1,2048]{2,0,1:T(8,128)S(1)}, u32[]{:S(2)}, u32[]{:S(2)}) %collective-permute-start.7) | collective-permute-done | bytes 131104 | tf_op jit(solution)/shard_map/ppermute | solution.py:21
  114.2 7.7 %all-reduce.29 = (f32[16]{0:T(128)S(1)}, f32[16]{0:T(128)S(1)}) all-reduce(f32[16]{0:T(128)S(1)} %get-tuple-element.15, f32[16]{0:T(128)S(1)} %get-tuple-element.14), channel_id=1, replica_groups=mesh['rows_0'=4,'rows_1'=4,'rows_2'=4,'rows_3'=2] {'rows_0'}, use_global_device_ids=true, to_apply=%region_21.22 | all-reduce | flops 32 | bytes 256 | tf_op jit(solution)/shard_map/psum | solution.py:27
  121.9 6.1 %all-reduce.21 = (f32[16]{0:T(128)S(1)}, f32[16]{0:T(128)S(1)}) all-reduce(f32[16]{0:T(128)S(1)} %get-tuple-element.62, f32[16]{0:T(128)S(1)} %get-tuple-element.63), channel_id=1, replica_groups=mesh['rows_0'=4,'rows_1'=4,'rows_2'=4,'rows_3'=2] {'rows_1'}, use_global_device_ids=true, to_apply=%region_22.23 | all-reduce | flops 32 | bytes 256 | tf_op jit(solution)/shard_map/psum | solution.py:27
  128.1 13.1 %all-reduce.13 = (f32[16]{0:T(128)S(1)}, f32[16]{0:T(128)S(1)}) all-reduce(f32[16]{0:T(128)S(1)} %get-tuple-element.46, f32[16]{0:T(128)S(1)} %get-tuple-element.47), channel_id=1, replica_groups=mesh['rows_0'=4,'rows_1'=4,'rows_2'=4,'rows_3'=2] {'rows_2'}, use_global_device_ids=true, to_apply=%region_23.24 | all-reduce | flops 32 | bytes 256 | tf_op jit(solution)/shard_map/psum | solution.py:27
  141.2 2.5 all-reduce.37
  145.3 3.8 collective-permute-start.8
  151.1 4.3 %collective-permute-done.9 = f32[16,1,2048]{2,0,1:T(8,128)S(1)} collective-permute-done((f32[16,1,2048]{2,0,1:T(8,128)S(1)}, f32[16,1,2048]{2,0,1:T(8,128)S(1)}, u32[]{:S(2)}, u32[]{:S(2)}) %collective-permute-start.9) | collective-permute-done | bytes 131104 | tf_op jit(solution)/shard_map/ppermute | solution.py:21
  156.4 6.5 %all-reduce.28 = (f32[16]{0:T(128)S(1)}, f32[16]{0:T(128)S(1)}) all-reduce(f32[16]{0:T(128)S(1)} %get-tuple-element.13, f32[16]{0:T(128)S(1)} %get-tuple-element.12), channel_id=1, replica_groups=mesh['rows_0'=4,'rows_1'=4,'rows_2'=4,'rows_3'=2] {'rows_0'}, use_global_device_ids=true, to_apply=%region_31.32 | all-reduce | flops 32 | bytes 256 | tf_op jit(solution)/shard_map/psum | solution.py:27
  162.9 7.3 %all-reduce.20 = (f32[16]{0:T(128)S(1)}, f32[16]{0:T(128)S(1)}) all-reduce(f32[16]{0:T(128)S(1)} %get-tuple-element.60, f32[16]{0:T(128)S(1)} %get-tuple-element.61), channel_id=1, replica_groups=mesh['rows_0'=4,'rows_1'=4,'rows_2'=4,'rows_3'=2] {'rows_1'}, use_global_device_ids=true, to_apply=%region_32.33 | all-reduce | flops 32 | bytes 256 | tf_op jit(solution)/shard_map/psum | solution.py:27
  170.2 12.9 %all-reduce.12 = (f32[16]{0:T(128)S(1)}, f32[16]{0:T(128)S(1)}) all-reduce(f32[16]{0:T(128)S(1)} %get-tuple-element.44, f32[16]{0:T(128)S(1)} %get-tuple-element.45), channel_id=1, replica_groups=mesh['rows_0'=4,'rows_1'=4,'rows_2'=4,'rows_3'=2] {'rows_2'}, use_global_device_ids=true, to_apply=%region_33.34 | all-reduce | flops 32 | bytes 256 | tf_op jit(solution)/shard_map/psum | solution.py:27
  183.1 2.5 all-reduce.36
  186.3 3.8 collective-permute-start.10
  190.1 1.9 collective-permute-start.11
  192.0 4.3 %collective-permute-done.11 = f32[16,1,2048]{2,0,1:T(8,128)S(1)} collective-permute-done((f32[16,1,2048]{2,0,1:T(8,128)S(1)}, f32[16,1,2048]{2,0,1:T(8,128)S(1)}, u32[]{:S(2)}, u32[]{:S(2)}) %collective-permute-start.11) | collective-permute-done | bytes 131104 | tf_op jit(solution)/shard_map/ppermute | solution.py:21
  197.4 6.4 %all-reduce.27 = (f32[16]{0:T(128)S(1)}, f32[16]{0:T(128)S(1)}) all-reduce(f32[16]{0:T(128)S(1)} %get-tuple-element.11, f32[16]{0:T(128)S(1)} %get-tuple-element.10), channel_id=1, replica_groups=mesh['rows_0'=4,'rows_1'=4,'rows_2'=4,'rows_3'=2] {'rows_0'}, use_global_device_ids=true, to_apply=%region_41.42 | all-reduce | flops 32 | bytes 256 | tf_op jit(solution)/shard_map/psum | solution.py:27
  203.8 7.4 %all-reduce.19 = (f32[16]{0:T(128)S(1)}, f32[16]{0:T(128)S(1)}) all-reduce(f32[16]{0:T(128)S(1)} %get-tuple-element.58, f32[16]{0:T(128)S(1)} %get-tuple-element.59), channel_id=1, replica_groups=mesh['rows_0'=4,'rows_1'=4,'rows_2'=4,'rows_3'=2] {'rows_1'}, use_global_device_ids=true, to_apply=%region_42.43 | all-reduce | flops 32 | bytes 256 | tf_op jit(solution)/shard_map/psum | solution.py:27
  211.2 12.6 %all-reduce.11 = (f32[16]{0:T(128)S(1)}, f32[16]{0:T(128)S(1)}) all-reduce(f32[16]{0:T(128)S(1)} %get-tuple-element.42, f32[16]{0:T(128)S(1)} %get-tuple-element.43), channel_id=1, replica_groups=mesh['rows_0'=4,'rows_1'=4,'rows_2'=4,'rows_3'=2] {'rows_2'}, use_global_device_ids=true, to_apply=%region_43.44 | all-reduce | flops 32 | bytes 256 | tf_op jit(solution)/shard_map/psum | solution.py:27
  223.8 2.5 all-reduce.35
  226.8 3.8 collective-permute-start.12
  230.7 2.1 collective-permute-start.13
  234.8 2.2 collective-permute-done.13
  238.8 6.7 %all-reduce.26 = (f32[16]{0:T(128)S(1)}, f32[16]{0:T(128)S(1)}) all-reduce(f32[16]{0:T(128)S(1)} %get-tuple-element.9, f32[16]{0:T(128)S(1)} %get-tuple-element.8), channel_id=1, replica_groups=mesh['rows_0'=4,'rows_1'=4,'rows_2'=4,'rows_3'=2] {'rows_0'}, use_global_device_ids=true, to_apply=%region_51.52 | all-reduce | flops 32 | bytes 256 | tf_op jit(solution)/shard_map/psum | solution.py:27
  245.5 7.1 %all-reduce.18 = (f32[16]{0:T(128)S(1)}, f32[16]{0:T(128)S(1)}) all-reduce(f32[16]{0:T(128)S(1)} %get-tuple-element.56, f32[16]{0:T(128)S(1)} %get-tuple-element.57), channel_id=1, replica_groups=mesh['rows_0'=4,'rows_1'=4,'rows_2'=4,'rows_3'=2] {'rows_1'}, use_global_device_ids=true, to_apply=%region_52.53 | all-reduce | flops 32 | bytes 256 | tf_op jit(solution)/shard_map/psum | solution.py:27
  252.6 12.6 %all-reduce.10 = (f32[16]{0:T(128)S(1)}, f32[16]{0:T(128)S(1)}) all-reduce(f32[16]{0:T(128)S(1)} %get-tuple-element.40, f32[16]{0:T(128)S(1)} %get-tuple-element.41), channel_id=1, replica_groups=mesh['rows_0'=4,'rows_1'=4,'rows_2'=4,'rows_3'=2] {'rows_2'}, use_global_device_ids=true, to_apply=%region_53.54 | all-reduce | flops 32 | bytes 256 | tf_op jit(solution)/shard_map/psum | solution.py:27
  265.2 2.5 all-reduce.34
  269.4 3.8 collective-permute-start.14
  273.3 1.9 collective-permute-start.15
  275.3 4.3 %collective-permute-done.15 = f32[16,1,2048]{2,0,1:T(8,128)S(1)} collective-permute-done((f32[16,1,2048]{2,0,1:T(8,128)S(1)}, f32[16,1,2048]{2,0,1:T(8,128)S(1)}, u32[]{:S(2)}, u32[]{:S(2)}) %collective-permute-start.15) | collective-permute-done | bytes 131104 | tf_op jit(solution)/shard_map/ppermute | solution.py:21
  281.4 6.7 %all-reduce.25 = (f32[16]{0:T(128)S(1)}, f32[16]{0:T(128)S(1)}) all-reduce(f32[16]{0:T(128)S(1)} %get-tuple-element.7, f32[16]{0:T(128)S(1)} %get-tuple-element.6), channel_id=1, replica_groups=mesh['rows_0'=4,'rows_1'=4,'rows_2'=4,'rows_3'=2] {'rows_0'}, use_global_device_ids=true, to_apply=%region_61.62 | all-reduce | flops 32 | bytes 256 | tf_op jit(solution)/shard_map/psum | solution.py:27
  288.1 7.1 %all-reduce.17 = (f32[16]{0:T(128)S(1)}, f32[16]{0:T(128)S(1)}) all-reduce(f32[16]{0:T(128)S(1)} %get-tuple-element.54, f32[16]{0:T(128)S(1)} %get-tuple-element.55), channel_id=1, replica_groups=mesh['rows_0'=4,'rows_1'=4,'rows_2'=4,'rows_3'=2] {'rows_1'}, use_global_device_ids=true, to_apply=%region_62.63 | all-reduce | flops 32 | bytes 256 | tf_op jit(solution)/shard_map/psum | solution.py:27
  295.2 12.6 %all-reduce.9 = (f32[16]{0:T(128)S(1)}, f32[16]{0:T(128)S(1)}) all-reduce(f32[16]{0:T(128)S(1)} %get-tuple-element.38, f32[16]{0:T(128)S(1)} %get-tuple-element.39), channel_id=1, replica_groups=mesh['rows_0'=4,'rows_1'=4,'rows_2'=4,'rows_3'=2] {'rows_2'}, use_global_device_ids=true, to_apply=%region_63.64 | all-reduce | flops 32 | bytes 256 | tf_op jit(solution)/shard_map/psum | solution.py:27
  307.8 2.5 all-reduce.33
  310.4 2.0 fusion.96
  312.4 3.8 collective-permute-start.16
  318.2 4.3 %collective-permute-done.17 = f32[16,1,2048]{2,0,1:T(8,128)S(1)} collective-permute-done((f32[16,1,2048]{2,0,1:T(8,128)S(1)}, f32[16,1,2048]{2,0,1:T(8,128)S(1)}, u32[]{:S(2)}, u32[]{:S(2)}) %collective-permute-start.17) | collective-permute-done | bytes 131104 | tf_op jit(solution)/shard_map/ppermute | solution.py:21
  323.5 6.7 %all-reduce.24 = (f32[16]{0:T(128)S(1)}, f32[16]{0:T(128)S(1)}) all-reduce(f32[16]{0:T(128)S(1)} %get-tuple-element.5, f32[16]{0:T(128)S(1)} %get-tuple-element.4), channel_id=1, replica_groups=mesh['rows_0'=4,'rows_1'=4,'rows_2'=4,'rows_3'=2] {'rows_0'}, use_global_device_ids=true, to_apply=%region_71.72 | all-reduce | flops 32 | bytes 256 | tf_op jit(solution)/shard_map/psum | solution.py:27
  330.2 7.1 %all-reduce.16 = (f32[16]{0:T(128)S(1)}, f32[16]{0:T(128)S(1)}) all-reduce(f32[16]{0:T(128)S(1)} %get-tuple-element.52, f32[16]{0:T(128)S(1)} %get-tuple-element.53), channel_id=1, replica_groups=mesh['rows_0'=4,'rows_1'=4,'rows_2'=4,'rows_3'=2] {'rows_1'}, use_global_device_ids=true, to_apply=%region_72.73 | all-reduce | flops 32 | bytes 256 | tf_op jit(solution)/shard_map/psum | solution.py:27
  337.3 12.6 %all-reduce.8 = (f32[16]{0:T(128)S(1)}, f32[16]{0:T(128)S(1)}) all-reduce(f32[16]{0:T(128)S(1)} %get-tuple-element.36, f32[16]{0:T(128)S(1)} %get-tuple-element.37), channel_id=1, replica_groups=mesh['rows_0'=4,'rows_1'=4,'rows_2'=4,'rows_3'=2] {'rows_2'}, use_global_device_ids=true, to_apply=%region_73.74 | all-reduce | flops 32 | bytes 256 | tf_op jit(solution)/shard_map/psum | solution.py:27
  349.9 2.5 all-reduce.32
  353.0 7.0 %fusion.7 = f32[48,256]{1,0:T(8,128)S(1)} fusion(bf16[256,4,2048]{2,1,0:T(4,128)(2,1)} %param.17, bf16[16,4,2048]{2,0,1:T(8,128)(2,1)S(1)} %multiply_convert_fusion, bf16[16,4,2048]{2,0,1:T(8,128)(2,1)} %copy.65, bf16[16,4,2048]{2,0,1:T(8,128)(2,1)} %copy.66), kind=kOutput, calls=%fused_computation.7 | convolution fusion | flops 203685888 | bytes 5029888 | tf_op jit(solution)/shard_map/cxy,rxy->cr/dot_general | solution.py:70
  360.0 12.2 %psum.540 = f32[48,256]{1,0:T(8,128)S(1)} all-reduce(f32[48,256]{1,0:T(8,128)S(1)} %fusion.7), channel_id=1, replica_groups=mesh['rows_0'=4,'rows_1'=4,'rows_2'=4,'rows_3'=2] {'rows_0'}, use_global_device_ids=true, to_apply=%region_80.81 | all-reduce | flops 12288 | bytes 98304 | tf_op jit(solution)/shard_map/psum | solution.py:27
  372.2 11.8 %psum.541 = f32[48,256]{1,0:T(8,128)S(1)} all-reduce(f32[48,256]{1,0:T(8,128)S(1)} %psum.540), channel_id=1, replica_groups=mesh['rows_0'=4,'rows_1'=4,'rows_2'=4,'rows_3'=2] {'rows_1'}, use_global_device_ids=true, to_apply=%region_81.82 | all-reduce | flops 12288 | bytes 98304 | tf_op jit(solution)/shard_map/psum | solution.py:27
  384.0 12.9 %psum.542 = f32[48,256]{1,0:T(8,128)S(1)} all-reduce(f32[48,256]{1,0:T(8,128)S(1)} %psum.541), channel_id=1, replica_groups=mesh['rows_0'=4,'rows_1'=4,'rows_2'=4,'rows_3'=2] {'rows_2'}, use_global_device_ids=true, to_apply=%region_82.83 | all-reduce | flops 12288 | bytes 98304 | tf_op jit(solution)/shard_map/psum | solution.py:27
  396.9 14.9 %psum.543 = f32[48,256]{1,0:T(8,128)S(1)} all-reduce(f32[48,256]{1,0:T(8,128)S(1)} %psum.542), channel_id=1, replica_groups=mesh['rows_0'=4,'rows_1'=4,'rows_2'=4,'rows_3'=2] {'rows_3'}, use_global_device_ids=true, to_apply=%region_83.84 | all-reduce | flops 12288 | bytes 98304 | tf_op jit(solution)/shard_map/psum | solution.py:27
  411.8 7.1 %fusion.4 = f32[16,4,2048]{2,0,1:T(8,128)S(1)} fusion(bf16[256,4,2048]{2,1,0:T(4,128)(2,1)} %param.17, f32[16,4,2048]{2,1,0:T(4,128)S(1)} %copy-done.6, f32[16,4,2048]{2,1,0:T(4,128)S(1)} %copy-done, f32[48,256]{1,0:T(8,128)S(1)} %psum.543, f32[16,256]{1,0:T(8,128)S(1)} %fusion.87), kind=kOutput, calls=%fused_computation.4 | convolution fusion | flops 67653632 | bytes 5816320 | tf_op jit(solution)/shard_map/cr,rxy->cxy/dot_general | solution.py:130
  (85 shorter events, 29.7 us)
Async XLA Ops:
  0.6 61.6 %copy-start = (f32[16,4,2048]{2,1,0:T(4,128)S(1)}, f32[16,4,2048]{2,1,0:T(4,128)}, u32[]{:S(2)}) copy-start(f32[16,4,2048]{2,1,0:T(4,128)} %param.13) | copy-start | bytes 1572868
  0.6 61.6 %copy-start.4 = (f32[4,2048]{1,0:T(4,128)S(1)}, f32[4,2048]{1,0:T(4,128)}, u32[]{:S(2)}) copy-start(f32[4,2048]{1,0:T(4,128)} %param.9) | copy-start | bytes 98308
  1.5 5.7 %collective-permute-start = (f32[1,2048]{1,0:T(1,128)S(1)}, f32[1,2048]{1,0:T(1,128)S(1)}, u32[]{:S(2)}, u32[]{:S(2)}) collective-permute-start(f32[1,2048]{1,0:T(1,128)S(1)} %slice.220), channel_id=1, source_target_pairs={{0,1},{1,2},{2,3},{3,4},{4,5},{5,6},{6,7},{7,8},{8,9},{9,10},{10,1... | collective-permute-start | bytes 24584 | tf_op jit(solution)/shard_map/ppermute | solution.py:20
  8.0 5.5 %collective-permute-start.1 = (f32[1,2048]{1,0:T(1,128)S(1)}, f32[1,2048]{1,0:T(1,128)S(1)}, u32[]{:S(2)}, u32[]{:S(2)}) collective-permute-start(f32[1,2048]{1,0:T(1,128)S(1)} %get-tuple-element.140), channel_id=1, source_target_pairs={{1,0},{2,1},{3,2},{4,3},{5,4},{6,5},{7,6},{8,7},{9,8},{10,9},{11,1... | collective-permute-start | bytes 24584 | tf_op jit(solution)/shard_map/ppermute | solution.py:21
  16.9 4.3 %collective-permute-start.2 = (f32[16,1,2048]{2,0,1:T(8,128)S(1)}, f32[16,1,2048]{2,0,1:T(8,128)S(1)}, u32[]{:S(2)}, u32[]{:S(2)}) collective-permute-start(f32[16,1,2048]{2,0,1:T(8,128)S(1)} %get-tuple-element.137), channel_id=1, source_target_pairs={{0,1},{1,2},{2,3},{3,4},{4,5},{5,6},{6,7},{7,8},{8,9},{9,10},{10,1... | collective-permute-start | bytes 393224 | tf_op jit(solution)/shard_map/ppermute | solution.py:20
  18.8 6.5 %collective-permute-start.3 = (f32[16,1,2048]{2,0,1:T(8,128)S(1)}, f32[16,1,2048]{2,0,1:T(8,128)S(1)}, u32[]{:S(2)}, u32[]{:S(2)}) collective-permute-start(f32[16,1,2048]{2,0,1:T(8,128)S(1)} %get-tuple-element.138), channel_id=1, source_target_pairs={{1,0},{2,1},{3,2},{4,3},{5,4},{6,5},{7,6},{8,7},{9,8},{10,9},{11,1... | collective-permute-start | bytes 393224 | tf_op jit(solution)/shard_map/ppermute | solution.py:21
  62.6 5.8 %collective-permute-start.4 = (f32[16,1,2048]{2,0,1:T(8,128)S(1)}, f32[16,1,2048]{2,0,1:T(8,128)S(1)}, u32[]{:S(2)}, u32[]{:S(2)}) collective-permute-start(f32[16,1,2048]{2,0,1:T(8,128)S(1)} %get-tuple-element.135), channel_id=1, source_target_pairs={{0,1},{1,2},{2,3},{3,4},{4,5},{5,6},{6,7},{7,8},{8,9},{9,10},{10,1... | collective-permute-start | bytes 393224 | tf_op jit(solution)/shard_map/ppermute | solution.py:20
  66.5 6.3 %collective-permute-start.5 = (f32[16,1,2048]{2,0,1:T(8,128)S(1)}, f32[16,1,2048]{2,0,1:T(8,128)S(1)}, u32[]{:S(2)}, u32[]{:S(2)}) collective-permute-start(f32[16,1,2048]{2,0,1:T(8,128)S(1)} %get-tuple-element.136), channel_id=1, source_target_pairs={{1,0},{2,1},{3,2},{4,3},{5,4},{6,5},{7,6},{8,7},{9,8},{10,9},{11,1... | collective-permute-start | bytes 393224 | tf_op jit(solution)/shard_map/ppermute | solution.py:21
  102.2 5.8 %collective-permute-start.6 = (f32[16,1,2048]{2,0,1:T(8,128)S(1)}, f32[16,1,2048]{2,0,1:T(8,128)S(1)}, u32[]{:S(2)}, u32[]{:S(2)}) collective-permute-start(f32[16,1,2048]{2,0,1:T(8,128)S(1)} %get-tuple-element.133), channel_id=1, source_target_pairs={{0,1},{1,2},{2,3},{3,4},{4,5},{5,6},{6,7},{7,8},{8,9},{9,10},{10,1... | collective-permute-start | bytes 393224 | tf_op jit(solution)/shard_map/ppermute | solution.py:20
  106.1 6.3 %collective-permute-start.7 = (f32[16,1,2048]{2,0,1:T(8,128)S(1)}, f32[16,1,2048]{2,0,1:T(8,128)S(1)}, u32[]{:S(2)}, u32[]{:S(2)}) collective-permute-start(f32[16,1,2048]{2,0,1:T(8,128)S(1)} %get-tuple-element.134), channel_id=1, source_target_pairs={{1,0},{2,1},{3,2},{4,3},{5,4},{6,5},{7,6},{8,7},{9,8},{10,9},{11,1... | collective-permute-start | bytes 393224 | tf_op jit(solution)/shard_map/ppermute | solution.py:21
  143.7 41.9 %copy-start.7 = (f32[4,2048]{1,0:T(4,128)S(1)}, f32[4,2048]{1,0:T(4,128)}, u32[]{:S(2)}) copy-start(f32[4,2048]{1,0:T(4,128)} %param.10) | copy-start | bytes 98308
  143.7 41.9 %copy-start.8 = (f32[4,2048]{1,0:T(4,128)S(1)}, f32[4,2048]{1,0:T(4,128)}, u32[]{:S(2)}) copy-start(f32[4,2048]{1,0:T(4,128)} %param.11) | copy-start | bytes 98308
  145.3 5.8 %collective-permute-start.8 = (f32[16,1,2048]{2,0,1:T(8,128)S(1)}, f32[16,1,2048]{2,0,1:T(8,128)S(1)}, u32[]{:S(2)}, u32[]{:S(2)}) collective-permute-start(f32[16,1,2048]{2,0,1:T(8,128)S(1)} %get-tuple-element.131), channel_id=1, source_target_pairs={{0,1},{1,2},{2,3},{3,4},{4,5},{5,6},{6,7},{7,8},{8,9},{9,10},{10,1... | collective-permute-start | bytes 393224 | tf_op jit(solution)/shard_map/ppermute | solution.py:20
  149.1 6.3 %collective-permute-start.9 = (f32[16,1,2048]{2,0,1:T(8,128)S(1)}, f32[16,1,2048]{2,0,1:T(8,128)S(1)}, u32[]{:S(2)}, u32[]{:S(2)}) collective-permute-start(f32[16,1,2048]{2,0,1:T(8,128)S(1)} %get-tuple-element.132), channel_id=1, source_target_pairs={{1,0},{2,1},{3,2},{4,3},{5,4},{6,5},{7,6},{8,7},{9,8},{10,9},{11,1... | collective-permute-start | bytes 393224 | tf_op jit(solution)/shard_map/ppermute | solution.py:21
  186.3 5.8 %collective-permute-start.10 = (f32[16,1,2048]{2,0,1:T(8,128)S(1)}, f32[16,1,2048]{2,0,1:T(8,128)S(1)}, u32[]{:S(2)}, u32[]{:S(2)}) collective-permute-start(f32[16,1,2048]{2,0,1:T(8,128)S(1)} %get-tuple-element.129), channel_id=1, source_target_pairs={{0,1},{1,2},{2,3},{3,4},{4,5},{5,6},{6,7},{7,8},{8,9},{9,10},{10,1... | collective-permute-start | bytes 393224 | tf_op jit(solution)/shard_map/ppermute | solution.py:20
  190.1 6.3 %collective-permute-start.11 = (f32[16,1,2048]{2,0,1:T(8,128)S(1)}, f32[16,1,2048]{2,0,1:T(8,128)S(1)}, u32[]{:S(2)}, u32[]{:S(2)}) collective-permute-start(f32[16,1,2048]{2,0,1:T(8,128)S(1)} %get-tuple-element.130), channel_id=1, source_target_pairs={{1,0},{2,1},{3,2},{4,3},{5,4},{6,5},{7,6},{8,7},{9,8},{10,9},{11,1... | collective-permute-start | bytes 393224 | tf_op jit(solution)/shard_map/ppermute | solution.py:21
  196.7 37.1 %copy-start.5 = (f32[16,4,2048]{2,1,0:T(4,128)S(1)}, f32[16,4,2048]{2,1,0:T(4,128)}, u32[]{:S(2)}) copy-start(f32[16,4,2048]{2,1,0:T(4,128)} %param.14) | copy-start | bytes 1572868
  197.4 70.4 %copy-start.1 = (f32[16,4,2048]{2,0,1:T(8,128)}, f32[16,4,2048]{2,0,1:T(8,128)S(1)}, u32[]{:S(2)}) copy-start(f32[16,4,2048]{2,0,1:T(8,128)S(1)} %get-tuple-element.102) | copy-start | bytes 1572868
  226.8 10.5 %copy-start.3 = (f32[16,4,2048]{2,0,1:T(8,128)}, f32[16,4,2048]{2,0,1:T(8,128)S(1)}, u32[]{:S(2)}) copy-start(f32[16,4,2048]{2,0,1:T(8,128)S(1)} %get-tuple-element.101) | copy-start | bytes 1572868
  226.8 8.0 %collective-permute-start.12 = (f32[16,1,2048]{2,0,1:T(8,128)S(1)}, f32[16,1,2048]{2,0,1:T(8,128)S(1)}, u32[]{:S(2)}, u32[]{:S(2)}) collective-permute-start(f32[16,1,2048]{2,0,1:T(8,128)S(1)} %get-tuple-element.127), channel_id=1, source_target_pairs={{0,1},{1,2},{2,3},{3,4},{4,5},{5,6},{6,7},{7,8},{8,9},{9,10},{10,1... | collective-permute-start | bytes 393224 | tf_op jit(solution)/shard_map/ppermute | solution.py:20
  230.7 6.3 %collective-permute-start.13 = (f32[16,1,2048]{2,0,1:T(8,128)S(1)}, f32[16,1,2048]{2,0,1:T(8,128)S(1)}, u32[]{:S(2)}, u32[]{:S(2)}) collective-permute-start(f32[16,1,2048]{2,0,1:T(8,128)S(1)} %get-tuple-element.128), channel_id=1, source_target_pairs={{1,0},{2,1},{3,2},{4,3},{5,4},{6,5},{7,6},{8,7},{9,8},{10,9},{11,1... | collective-permute-start | bytes 393224 | tf_op jit(solution)/shard_map/ppermute | solution.py:21
  234.8 40.4 %copy-start.11 = (f32[256]{0:T(256)S(1)}, f32[256]{0:T(256)}, u32[]{:S(2)}) copy-start(f32[256]{0:T(256)} %param.16) | copy-start | bytes 3076
  269.4 10.5 %copy-start.2 = (f32[16,4,2048]{2,0,1:T(8,128)}, f32[16,4,2048]{2,0,1:T(8,128)S(1)}, u32[]{:S(2)}) copy-start(f32[16,4,2048]{2,0,1:T(8,128)S(1)} %get-tuple-element.95) | copy-start | bytes 1572868
  269.4 5.8 %collective-permute-start.14 = (f32[16,1,2048]{2,0,1:T(8,128)S(1)}, f32[16,1,2048]{2,0,1:T(8,128)S(1)}, u32[]{:S(2)}, u32[]{:S(2)}) collective-permute-start(f32[16,1,2048]{2,0,1:T(8,128)S(1)} %get-tuple-element.125), channel_id=1, source_target_pairs={{0,1},{1,2},{2,3},{3,4},{4,5},{5,6},{6,7},{7,8},{8,9},{9,10},{10,1... | collective-permute-start | bytes 393224 | tf_op jit(solution)/shard_map/ppermute | solution.py:20
  273.3 6.3 %collective-permute-start.15 = (f32[16,1,2048]{2,0,1:T(8,128)S(1)}, f32[16,1,2048]{2,0,1:T(8,128)S(1)}, u32[]{:S(2)}, u32[]{:S(2)}) collective-permute-start(f32[16,1,2048]{2,0,1:T(8,128)S(1)} %get-tuple-element.126), channel_id=1, source_target_pairs={{1,0},{2,1},{3,2},{4,3},{5,4},{6,5},{7,6},{8,7},{9,8},{10,9},{11,1... | collective-permute-start | bytes 393224 | tf_op jit(solution)/shard_map/ppermute | solution.py:21
  312.4 5.8 %collective-permute-start.16 = (f32[16,1,2048]{2,0,1:T(8,128)S(1)}, f32[16,1,2048]{2,0,1:T(8,128)S(1)}, u32[]{:S(2)}, u32[]{:S(2)}) collective-permute-start(f32[16,1,2048]{2,0,1:T(8,128)S(1)} %get-tuple-element.123), channel_id=1, source_target_pairs={{0,1},{1,2},{2,3},{3,4},{4,5},{5,6},{6,7},{7,8},{8,9},{9,10},{10,1... | collective-permute-start | bytes 393224 | tf_op jit(solution)/shard_map/ppermute | solution.py:20
  316.2 6.3 %collective-permute-start.17 = (f32[16,1,2048]{2,0,1:T(8,128)S(1)}, f32[16,1,2048]{2,0,1:T(8,128)S(1)}, u32[]{:S(2)}, u32[]{:S(2)}) collective-permute-start(f32[16,1,2048]{2,0,1:T(8,128)S(1)} %get-tuple-element.124), channel_id=1, source_target_pairs={{1,0},{2,1},{3,2},{4,3},{5,4},{6,5},{7,6},{8,7},{9,8},{10,9},{11,1... | collective-permute-start | bytes 393224 | tf_op jit(solution)/shard_map/ppermute | solution.py:21
  353.0 58.8 %copy-start.10 = (f32[16,256]{1,0:T(8,128)S(1)}, f32[16,256]{1,0:T(8,128)}, u32[]{:S(2)}) copy-start(f32[16,256]{1,0:T(8,128)} %param.15) | copy-start | bytes 49156
  353.0 58.9 %copy-start.6 = (f32[16,4,2048]{2,1,0:T(4,128)S(1)}, f32[16,4,2048]{2,1,0:T(4,128)}, u32[]{:S(2)}) copy-start(f32[16,4,2048]{2,1,0:T(4,128)} %param.14) | copy-start | bytes 1572868
  411.8 8.3 %copy-start.9 = (f32[16,256]{1,0:T(8,128)}, f32[16,256]{1,0:T(8,128)S(1)}, u32[]{:S(2)}) copy-start(f32[16,256]{1,0:T(8,128)S(1)} %fusion.87) | copy-start | bytes 49156
where the time goes:
time: 422 us; the launch traced here: 420 us
  blocking collectives  289 us (68%)
  starting transfers between devices  51.8 us (12%)
  waiting for transfers between devices  36.7 us (9%)
  other arithmetic  22.8 us (5%)
  matrix products  14.1 us (3%)
    psum x36, blocking collectives, one_axis_at_a_time(): return functools.reduce(lax.psum, axes, value)  289 us
    ppermute x9, waiting for transfers between devices, extended(): after = lax.ppermute(leading, axis, down)  36 us
    ppermute x9, starting transfers between devices, extended(): before = lax.ppermute(last, axis, up)  33.8 us
    ppermute x9, starting transfers between devices, extended(): after = lax.ppermute(leading, axis, down)  17.9 us
    reduce_sum x8, other arithmetic, chain_dot(): return jnp.sum(left * right, axis=(1, 2))  8.94 us
  transfers between devices with their start and end apart: 18, of which 10 were waited for; matrix products, arithmetic and copies ran while one was open for 0% of the time, Pallas kernels for 0%

commit v1 on v0

v1 whole, which is shorter than its diff:
```python
import functools

import jax
import jax.numpy as jnp
from jax import lax
from jax.experimental import pallas as pl
from jax.experimental.pallas import tpu as pltpu
from jax.sharding import PartitionSpec as P

ITERS = 4
AXIS = "rows"
N = 128
RD = 4
NY = 2048
CH = 16
EXT = 12
TILES = NY // 128
MESH_ID = pl.DeviceIdType.MESH
F32 = jnp.float32


def greet_all(me):
    barrier = pltpu.get_barrier_semaphore()

    def signal(step, carry):
        pl.semaphore_signal(barrier, inc=1, device_id=(lax.rem(me + step, N),), device_id_type=MESH_ID)
        return carry

    lax.fori_loop(1, N, signal, 0)
    return barrier


def send_row_to_all(me, buf, send_sem, recv_sem):
    def send(step, carry):
        pltpu.make_async_remote_copy(
            src_ref=buf.at[me], dst_ref=buf.at[me], send_sem=send_sem, recv_sem=recv_sem,
            device_id=(lax.rem(me + step, N),), device_id_type=MESH_ID,
        ).start()
        return carry

    lax.fori_loop(1, N, send, 0, unroll=8)


def wait_rows(buf, sem):
    part = buf.at[pl.ds(0, N - 1)]
    pltpu.make_async_copy(part, part, sem).wait()


def pack(accs):
    lane = lax.broadcasted_iota(jnp.int32, (8, 128), 1)
    sub = lax.broadcasted_iota(jnp.int32, (8, 128), 0)
    row = jnp.zeros((8, 128), F32)
    for k in range(8):
        for g in range(2):
            total = jnp.sum(accs[k][g], axis=1, keepdims=True)
            row = row + jnp.where(lane == (g * 8 + k) * 8 + sub, total, 0.0)
    return jnp.sum(row, axis=0, keepdims=True)


def unpack(row):
    lane = lax.broadcasted_iota(jnp.int32, (8, 128), 1)
    sub = lax.broadcasted_iota(jnp.int32, (8, 128), 0)
    wide = jnp.broadcast_to(row, (8, 128))
    moments = []
    for k in range(8):
        halves = [
            jnp.sum(jnp.where(lane == (g * 8 + k) * 8 + sub, wide, 0.0), axis=1, keepdims=True)
            for g in range(2)
        ]
        moments.append(jnp.concatenate(halves, axis=0))
    return moments


def square(poly):
    out = [None] * (2 * len(poly) - 1)
    for i, a in enumerate(poly):
        for j, b in enumerate(poly):
            term = a * b
            out[i + j] = term if out[i + j] is None else out[i + j] + term
    return out


def krylov_weights(m):
    one = jnp.ones_like(m[0])
    rho, pi = [one], [one]
    y = [jnp.zeros_like(one)] * ITERS
    g = m[0]
    spread = g
    gain, noise = None, None
    for step in range(ITERS):
        s = square(pi)
        c = functools.reduce(lambda a, b: a + b, [s[l] * (m[l] - m[l + 1]) for l in range(len(s))])
        size = functools.reduce(
            lambda a, b: a + b, [jnp.abs(s[l]) * (jnp.abs(m[l]) + jnp.abs(m[l + 1])) for l in range(len(s))]
        )
        alpha = g / c
        part = alpha * g
        err = part * ((size / c) * (size / c) + (spread / g) * (spread / g))
        gain = part if gain is None else gain + part
        noise = err if noise is None else noise + err
        for k in range(len(pi)):
            y[k] = y[k] + alpha * pi[k]
        if step == ITERS - 1:
            break
        new = []
        for k in range(len(pi) + 1):
            value = rho[k] if k < len(rho) else None
            if k < len(pi):
                value = value - alpha * pi[k]
            if k > 0:
                moved = alpha * pi[k - 1]
                value = moved if value is None else value + moved
            new.append(value)
        rho = new
        s = square(rho)
        following = functools.reduce(lambda a, b: a + b, [s[l] * m[l] for l in range(len(s))])
        spread = functools.reduce(lambda a, b: a + b, [jnp.abs(s[l]) * jnp.abs(m[l]) for l in range(len(s))])
        beta = following / g
        g = following
        pi = [rho[k] + beta * pi[k] if k < len(pi) else rho[k] for k in range(len(rho))]
    return y, noise / gain


def apply_row(vk, vn, wu, wl, dinv, e, g, lane, accs, store):
    gs = pl.ds(8 * g, 8)

    def tile(ref, row, j, rows=gs):
        return ref[row, rows, pl.ds(128 * j, 128)]

    whole = pl.ds(0, 8)
    v_at = {}
    q_at = {}
    r_at = {}
    rq_at = {}

    def prepare(j):
        v = tile(vk, e, j)
        w = tile(wl, e, j, whole)
        v_at[j] = v
        q_at[j] = w
        r_at[j] = pltpu.roll(v, 1, 1)
        rq_at[j] = pltpu.roll(w * v, 127, 1)

    prepare(0)
    for j in range(TILES):
        if j + 1 < TILES:
            prepare(j + 1)
        left = r_at[j] if j == 0 else jnp.where(lane == 0, r_at[j - 1], r_at[j])
        right = jnp.where(lane == 127, rq_at[j + 1] if j + 1 < TILES else 0.0, rq_at[j])
        t = tile(wu, e, j, whole) * tile(vk, e - 1, j) + tile(wu, e + 1, j, whole) * tile(vk, e + 1, j)
        t = t + (q_at[j] * left + right)
        v = v_at[j]
        if accs is not None:
            accs = (accs[0] + t * v, accs[1])
        if store:
            new = t * tile(dinv, e, j)
            vn[e, gs, pl.ds(128 * j, 128)] = new
            if accs is not None:
                accs = (accs[0], accs[1] + t * new)
    return accs


def powers_own(v, k, wu, wl, dinv, lane):
    zero = jnp.zeros((8, 128), F32)
    store = k < ITERS - 1
    vk = v.at[k]
    vn = v.at[k + 1] if store else None

    def row(e, carry):
        return tuple(apply_row(vk, vn, wu, wl, dinv, e, g, lane, carry[g], store) for g in range(2))

    got = lax.fori_loop(RD, 2 * RD, row, ((zero, zero), (zero, zero)))
    return [got[0][0], got[1][0]], [got[0][1], got[1][1]]


def powers_halo(v, k, wu, wl, dinv, lane, lo, hi):
    vk, vn = v.at[k], v.at[k + 1]

    def row(i, carry):
        for e in (i, EXT - 1 - i):
            for g in range(2):
                apply_row(vk, vn, wu, wl, dinv, e, g, lane, None, True)
        return carry

    lax.fori_loop(lo, hi, row, 0)


def field_kernel(
    source, observed, precision, conductivity, log_rows, grad_ref, info_ref,
    lf, dinv, v, wu, wl, ws, sx, ox, px, state, cb, sb, ob, pb, mom_a, mom_b,
    local_sem, send_sem, recv_sem, all_sem,
):
    me = lax.axis_index(AXIS)
    own = [
        pltpu.make_async_copy(log_rows, lf.at[pl.ds(RD, RD)], local_sem.at[0]),
        pltpu.make_async_copy(conductivity, cb.at[2], local_sem.at[1]),
        pltpu.make_async_copy(source, sb.at[1], local_sem.at[2]),
        pltpu.make_async_copy(observed, ob.at[1], local_sem.at[3]),
        pltpu.make_async_copy(precision, pb.at[1], local_sem.at[4]),
    ]
    for copy in own:
        copy.start()
    barrier = greet_all(me)
    for copy in own:
        copy.wait()
    pl.semaphore_wait(barrier, N - 1)

    count = [0]

    def remote(src, dst, shift):
        index = count[0]
        count[0] += 1
        copy = pltpu.make_async_remote_copy(
            src_ref=src, dst_ref=dst, send_sem=send_sem.at[index], recv_sem=recv_sem.at[index],
            device_id=(lax.rem(me + shift + N, N),), device_id_type=MESH_ID,
        )
        copy.start()
        return copy

    early = []
    for block, src, centre in ((cb, 2, 2), (sb, 1, 1)):
        early.append(remote(block.at[src], block.at[centre - 1], 1))
        early.append(remote(block.at[src], block.at[centre + 1], -1))
    early.append(remote(cb.at[2], cb.at[0], 2))
    early.append(remote(cb.at[2], cb.at[4], -2))
    rows = []
    for i in range(RD):
        rows.append(
            (
                remote(lf.at[2 * RD - 1 - i], lf.at[RD - 1 - i], 1),
                remote(lf.at[RD + i], lf.at[2 * RD + i], -1),
            )
        )
    late = []
    for block in (ob, pb):
        late.append(remote(block.at[1], block.at[0], 1))
        late.append(remote(block.at[1], block.at[2], -1))

    for copy in early:
        copy.wait()

    lane = lax.broadcasted_iota(jnp.int32, (8, 128), 1)
    first = jnp.where(me == 0, 0.0, 1.0).astype(F32)
    last = jnp.where(me == N - 1, 0.0, 1.0).astype(F32)
    col = lax.broadcasted_iota(jnp.int32, (1, NY), 1)

    def crow(e):
        return cb[e // RD + 1, pl.ds(e % RD, 1), :]

    def edge(e):
        a, b = crow(e - 1), crow(e)
        if e == RD:
            a = first * a + (1.0 - first) * b
        if e == 2 * RD:
            b = last * b + (1.0 - last) * a
        return 0.5 * (a + b)

    for e in range(EXT + 1):
        wu[e] = jnp.broadcast_to(edge(e), (8, NY))
    for e in range(EXT):
        c = crow(e)
        before = jnp.where(col == 0, c, pltpu.roll(c, 1, 1))
        after = jnp.where(col == NY - 1, c, pltpu.roll(c, NY - 1, 1))
        left = 0.5 * (c + before)
        right = 0.5 * (c + after)
        wl[e] = jnp.broadcast_to(jnp.where(col == 0, 0.0, left), (8, NY))
        ws[e] = jnp.broadcast_to(left + right, (8, NY)) + wu[e] + wu[e + 1]
        sx[e] = jnp.broadcast_to(sb[e // RD, pl.ds(e % RD, 1), :], (8, NY))

    def start_row(e, keep):
        for g in range(2):
            gs = pl.ds(8 * g, 8)
            d = keep / (ws[e] + jnp.exp(lf[e, gs, :]))
            dinv[e, gs, :] = d
            v[0, e, gs, :] = sx[e] * d

    def own_start(e, carry):
        start_row(e, jnp.float32(1.0))
        return carry

    lax.fori_loop(RD, 2 * RD, own_start, 0)
    for i, (above, below) in enumerate(rows):
        above.wait()
        below.wait()
        start_row(RD - 1 - i, first)
        start_row(2 * RD + i, last)

    def moments_zero(side):
        zero = jnp.zeros((8, 128), F32)

        def row(e, carry):
            out = []
            for g in range(2):
                acc = carry[g]
                for j in range(TILES):
                    sl = pl.ds(128 * j, 128)
                    acc = acc + side(e, g, sl) * v[0, e, pl.ds(8 * g, 8), sl]
                out.append(acc)
            return tuple(out)

        return list(lax.fori_loop(RD, 2 * RD, row, (zero, zero)))

    accs = [moments_zero(lambda e, g, sl: sx[e, :, sl])]
    moved = []
    for k in range(ITERS):
        one, two = powers_own(v, k, wu, wl, dinv, lane)
        accs.append(one)
        if k < ITERS - 1:
            accs.append(two)
            moved.append(remote(v.at[k + 1, RD], v.at[k + 1, 0], 1))
            moved.append(remote(v.at[k + 1, 2 * RD - 1], v.at[k + 1, EXT - 1], -1))
            powers_halo(v, k, wu, wl, dinv, lane, k + 1, RD)
    mom_a[me] = pack(accs)
    send_row_to_all(me, mom_a, all_sem.at[0], all_sem.at[1])

    for copy in late:
        copy.wait()
    for e in range(EXT):
        ox[e] = jnp.broadcast_to(ob[e // RD, pl.ds(e % RD, 1), :], (8, NY))
        px[e] = jnp.broadcast_to(pb[e // RD, pl.ds(e % RD, 1), :], (8, NY))
    moved[0].wait()
    moved[1].wait()
    powers_halo(v, 1, wu, wl, dinv, lane, 1, 2)
    moved[2].wait()
    moved[3].wait()
    powers_halo(v, 2, wu, wl, dinv, lane, 1, 3)
    moved[4].wait()
    moved[5].wait()

    wait_rows(mom_a, all_sem.at[1])
    y, info = krylov_weights(unpack(jnp.sum(mom_a[...], axis=0)))
    info_ref[0] = jnp.broadcast_to(info, (CH, 128))

    def adjoint_start(e, carry):
        out = []
        for g in range(2):
            acc = carry[g]
            gs = pl.ds(8 * g, 8)
            yg = [jnp.broadcast_to(y[k][8 * g:8 * g + 8], (8, 128)) for k in range(ITERS)]
            for j in range(TILES):
                sl = pl.ds(128 * j, 128)
                x = yg[0] * v[0, e, gs, sl]
                for k in range(1, ITERS):
                    x = x + yg[k] * v[k, e, gs, sl]
                side = px[e, :, sl] * (x - ox[e, :, sl])
                new = side * dinv[e, gs, sl]
                state[e, gs, sl] = x
                v[0, e, gs, sl] = new
                acc = acc + side * new
            out.append(acc)
        return tuple(out)

    zero = jnp.zeros((8, 128), F32)
    lax.fori_loop(0, RD, adjoint_start, (zero, zero))
    lax.fori_loop(2 * RD, EXT, adjoint_start, (zero, zero))
    accs = [list(lax.fori_loop(RD, 2 * RD, adjoint_start, (zero, zero)))]
    for k in range(ITERS):
        one, two = powers_own(v, k, wu, wl, dinv, lane)
        accs.append(one)
        if k < ITERS - 1:
            accs.append(two)
            powers_halo(v, k, wu, wl, dinv, lane, k + 1, RD)
    mom_b[me] = pack(accs)
    send_row_to_all(me, mom_b, all_sem.at[2], all_sem.at[3])
    wait_rows(mom_b, all_sem.at[3])
    y, info = krylov_weights(unpack(jnp.sum(mom_b[...], axis=0)))
    info_ref[1] = jnp.broadcast_to(info, (CH, 128))

    def gradient(r, carry):
        for h in range(4):
            sl = pl.ds(512 * h, 512)
            adj = y[0] * v[0, r + RD, :, sl]
            for k in range(1, ITERS):
                adj = adj + y[k] * v[k, r + RD, :, sl]
            value = -jnp.exp(lf[r + RD, :, sl]) * adj * state[r + RD, :, sl]
            grad_ref[r, :, sl] = value.astype(jnp.bfloat16)
        return carry

    lax.fori_loop(0, RD, gradient, 0)
    wait_rows(mom_a, all_sem.at[0])
    wait_rows(mom_b, all_sem.at[2])


def solve_fields(source, observed, precision, conductivity, log_rows):
    any_space = pl.BlockSpec(memory_space=pl.ANY)
    vmem = pl.BlockSpec(memory_space=pltpu.VMEM)
    wide = pltpu.VMEM((EXT, CH, NY), F32)
    row8 = pltpu.VMEM((EXT, 8, NY), F32)
    small = pltpu.VMEM((3, RD, NY), F32)
    return pl.pallas_call(
        field_kernel,
        out_shape=(
            jax.ShapeDtypeStruct((RD, CH, NY), jnp.bfloat16),
            jax.ShapeDtypeStruct((2, CH, 128), F32),
        ),
        in_specs=[any_space] * 5,
        out_specs=(vmem, vmem),
        scratch_shapes=[
            wide, wide, pltpu.VMEM((ITERS, EXT, CH, NY), F32),
            pltpu.VMEM((EXT + 1, 8, NY), F32), row8, row8, row8, row8, row8, wide,
            pltpu.VMEM((5, RD, NY), F32), small, small, small,
            pltpu.VMEM((N, 1, 128), F32), pltpu.VMEM((N, 1, 128), F32),
            pltpu.SemaphoreType.DMA((5,)),
            pltpu.SemaphoreType.DMA((24,)),
            pltpu.SemaphoreType.DMA((24,)),
            pltpu.SemaphoreType.DMA((4,)),
        ],
        compiler_params=pltpu.CompilerParams(
            collective_id=0, has_side_effects=True, vmem_limit_bytes=40 << 20
        ),
    )(source, observed, precision, conductivity, log_rows)


def sum_kernel(part, total, got, mine, sems):
    me = lax.axis_index(AXIS)
    barrier = greet_all(me)
    pl.semaphore_wait(barrier, N - 1)

    def send(step, carry):
        to = lax.rem(me + step, N)
        pltpu.make_async_remote_copy(
            src_ref=part.at[to], dst_ref=got.at[me], send_sem=sems.at[0], recv_sem=sems.at[1],
            device_id=(to,), device_id_type=MESH_ID,
        ).start()
        return carry

    lax.fori_loop(1, N, send, 0, unroll=8)
    got[me] = part[me]
    wait_rows(got, sems.at[1])
    mine[me] = jnp.sum(got[...], axis=0)
    send_row_to_all(me, mine, sems.at[2], sems.at[3])
    wait_rows(mine, sems.at[3])
    total[...] = mine[...]
    wait_rows(got, sems.at[0])
    wait_rows(mine, sems.at[2])


def sum_all(coefs):
    flat = jnp.pad(coefs.reshape(N, 1, -1), ((0, 0), (0, 0), (0, 32)))
    vmem = pl.BlockSpec(memory_space=pltpu.VMEM)
    total = pl.pallas_call(
        sum_kernel,
        out_shape=jax.ShapeDtypeStruct((N, 1, 128), F32),
        in_specs=[vmem],
        out_specs=vmem,
        scratch_shapes=[
            pltpu.VMEM((N, 1, 128), F32), pltpu.VMEM((N, 1, 128), F32), pltpu.SemaphoreType.DMA((4,)),
        ],
        compiler_params=pltpu.CompilerParams(collective_id=1, has_side_effects=True),
    )(flat)
    return total[:, :, :96].reshape(coefs.shape)


def per_device(
    source, observed, precision, conductivity, log_field, noise_field, subspace_noise, eigenvalues, basis,
):
    log_rows = jnp.transpose(log_field, (1, 0, 2))
    gradient, info = solve_fields(source, observed, precision, conductivity, log_rows)
    gradient = jnp.transpose(gradient, (1, 0, 2))
    stacked = jnp.concatenate(
        [log_field.astype(jnp.bfloat16), noise_field.astype(jnp.bfloat16), gradient], 0
    )
    part = jnp.einsum("cxy,rxy->cr", stacked, basis, preferred_element_type=F32)
    coefs = sum_all(part)
    state_coef, noise_coef, grad_coef = coefs[:CH], coefs[CH : 2 * CH], coefs[2 * CH :]
    variance = 1.0 / (1.0 + eigenvalues)
    keep_factor = (2.0 - 0.8 * variance) / (2.0 + 0.8 * variance)
    drift_factor = 1.6 * variance / (2.0 + 0.8 * variance)
    noise_factor = jnp.sqrt(6.4 * variance) / (2.0 + 0.8 * variance)
    new_coef = keep_factor * state_coef - drift_factor * grad_coef + noise_factor * subspace_noise
    correction = (new_coef - 0.6 * state_coef - 0.8 * noise_coef).astype(jnp.bfloat16)
    rebuilt = jnp.einsum("cr,rxy->cxy", correction, basis, preferred_element_type=F32)
    proposal = 0.6 * log_field + 0.8 * noise_field + rebuilt
    return (proposal, new_coef)


def solution(mesh):
    return jax.shard_map(
        per_device,
        mesh=mesh,
        in_specs=(
            P(AXIS, None), P(AXIS, None), P(AXIS, None), P(AXIS, None),
            P(None, AXIS, None), P(None, AXIS, None), P(), P(), P(None, AXIS, None),
        ),
        out_specs=(P(None, AXIS, None), P()),
        check_vma=False,
    )
```

time: 422 us -> 96.7 us (0.23)
  blocking collectives: 289 us -> 0 us
  Pallas kernels: 0 us -> 70.5 us
  starting transfers between devices: 51.8 us -> 0 us
  waiting for transfers between devices: 36.7 us -> 0 us
  other arithmetic: 22.8 us -> 0.7 us
  local copies, waits for them, and re-layouts: 4.17 us -> 10.2 us
    psum x36 -> x0, blocking collectives: 289 us -> none  [one_axis_at_a_time(): return functools.reduce(lax.psum, axes, value)]
    pallas_call x0 -> x2, Pallas kernels: none -> 70.5 us  [the longest x1 51.2 us: solve_fields(): pl.pallas_call(field_kernel, out_shape=(jax.ShapeDtypeStruct((RD, CH, NY)...]
    ppermute x18 -> x0, starting transfers between devices: 51.8 us -> none  [the longest x9 33.8 us: extended(): before = lax.ppermute(last, axis, up)]
    ppermute x18 -> x0, waiting for transfers between devices: 36.7 us -> none  [the longest x9 36 us: extended(): after = lax.ppermute(leading, axis, down)]
    reduce_sum x8 -> x0, other arithmetic: 8.94 us -> none  [chain_dot(): return jnp.sum(left * right, axis=(1, 2))]
    div x16 -> x0, other arithmetic: 8.42 us -> none  [the longest x6 6.34 us: solve_paired(): scaled = residual / diagonal]
    unnamed x27 -> x20, local copies, waits for them, and re-layouts: 3.19 us -> 8.29 us
  transfers between devices with their start and end apart: 18 -> 0, of which waited for: 10 -> 0; matrix products, arithmetic and copies ran while one was open for 0% -> 0% of each run, Pallas kernels for 0% -> 0%
where the time goes in v1:
time: 96.7 us; the launch traced here: 96 us
  Pallas kernels  70.5 us (73%)
  matrix products  13.9 us (14%)
  local copies, waits for them, and re-layouts  10.2 us (11%)
    pallas_call x1, Pallas kernels, solve_fields(): pl.pallas_call(field_kernel, out_shape=(jax.ShapeDtypeStruct((RD, CH, NY)...  51.2 us
    pallas_call x1, Pallas kernels, sum_all(): pl.pallas_call(sum_kernel, out_shape=jax.ShapeDtypeStruct((N, 1, 128), F3...  19.3 us
    unnamed x20, local copies, waits for them, and re-layouts  8.29 us
    dot_general x1, matrix products, per_device(): jnp.einsum('cr,rxy->cxy', correction, basis, preferred_element_type=F32)  7.15 us
    dot_general x1, matrix products, per_device(): part = jnp.einsum('cxy,rxy->cr', stacked, basis, preferred_element_type=F32)  6.75 us

profile of v1, /device:TPU:1, one launch (start us, length us, event | category | flops | bytes accessed | tf_op | source)
XLA Modules:
  0.0 96.0 jit_solution(15917943004697488276)
XLA Ops:
  0.6 0.7 subtract_divide_fusion
  1.3 1.4 %copy.43 = f32[16,4,2048]{2,0,1:T(8,128)S(1)} copy(f32[16,4,2048]{2,1,0:T(4,128)} %param.13) | data formatting | bytes 1048576 | tf_op args[4]
  2.7 0.0 copy-start
  2.7 0.7 copy-done
  3.5 0.0 copy-start.1
  3.5 0.8 copy-done.1
  4.2 0.0 copy-start.2
  4.2 0.8 copy-done.2
  5.0 0.0 copy-start.3
  5.0 0.8 copy-done.3
  5.7 51.2 %shard_map.104 = (bf16[4,16,2048]{2,1,0:T(8,128)(2,1)S(1)}, f32[2,16,128]{2,1,0:T(8,128)}) custom-call(f32[4,2048]{1,0:T(4,128)S(1)} %copy-done, f32[4,2048]{1,0:T(4,128)S(1)} %copy-done.1, f32[4,2048]{1,0:T(4,128)S(1)} %copy-done.2, f32[4,2048]{1,0:T(4,128)S(1)} %copy-done.3, f32[4,16,2048]{2,1,0:T(8,128)S(1)} %bitcast.10), custom_call_target="tpu_custom_call" | custom-call | tf_op jit(solution)/shard_map/pallas_call | solution.py:390
  56.9 1.3 %copy.41 = bf16[16,4,2048]{2,0,1:T(8,128)(2,1)S(1)} copy(f32[16,4,2048]{2,1,0:T(4,128)} %param.14) | data formatting | bytes 786432 | tf_op args[5]
  58.2 0.0 copy-start.7
  58.2 0.0 copy-start.4
  58.3 0.0 copy-start.5
  58.3 1.4 %copy.42 = bf16[16,4,2048]{2,0,1:T(8,128)(2,1)S(1)} copy(f32[16,4,2048]{2,1,0:T(4,128)} %param.13) | data formatting | bytes 786432 | tf_op args[4]
  59.7 6.7 %fusion.7 = f32[48,256]{1,0:T(8,128)S(1)} fusion(bf16[256,4,2048]{2,1,0:T(4,128)(2,1)} %param.17, bf16[16,4,2048]{2,0,1:T(8,128)(2,1)S(1)} %bitcast.11, bf16[16,4,2048]{2,0,1:T(8,128)(2,1)S(1)} %copy.41, bf16[16,4,2048]{2,0,1:T(8,128)(2,1)S(1)} %copy.42), kind=kOutput, calls=%fused_computation.5 | convolution fusion | flops 203685888 | bytes 5029888 | tf_op jit(solution)/shard_map/cxy,rxy->cr/dot_general | solution.py:463
  66.4 0.1 reshape.13
  66.5 0.7 pad.4.part
  67.2 19.3 %shard_map.105 = f32[128,1,128]{2,1,0:T(1,128)} custom-call(f32[128,1,128]{2,1,0:T(1,128)} %pad.4.part), custom_call_target="tpu_custom_call" | custom-call | tf_op jit(solution)/shard_map/pallas_call | solution.py:441
  86.5 1.0 %slice_reduce_fusion = f32[128,96]{1,0:T(8,128)S(1)} fusion(f32[128,1,128]{2,1,0:T(1,128)} %shard_map.105), kind=kLoop, calls=%fused_computation.14 | loop fusion | bytes 98304 | tf_op jit(solution)/shard_map/slice | solution.py:451
  87.5 0.1 reshape.14
  87.6 0.0 copy-done.7
  87.6 0.0 copy-done.4
  87.7 0.0 copy-done.5
  87.7 0.0 copy-start.6
  87.7 7.1 %fusion.4 = f32[16,4,2048]{2,0,1:T(8,128)S(1)} fusion(bf16[256,4,2048]{2,1,0:T(4,128)(2,1)} %param.17, f32[16,4,2048]{2,1,0:T(4,128)S(1)} %copy-done.5, f32[16,4,2048]{2,1,0:T(4,128)S(1)} %copy-done.4, f32[48,256]{1,0:T(8,128)S(1)} %reshape.14, f32[16,256]{1,0:T(8,128)S(1)} %fusion.18), kind=kOutput, calls=%fused_computation.4 | convolution fusion | flops 67653632 | bytes 5816320 | tf_op jit(solution)/shard_map/cr,rxy->cxy/dot_general | solution.py:472
  94.8 1.1 %copy.27 = f32[16,4,2048]{2,1,0:T(4,128)} copy(f32[16,4,2048]{2,0,1:T(8,128)S(1)} %fusion.4) | data formatting | bytes 1048576
  96.0 0.0 copy-done.6
  (2 shorter events, 0.0 us)
Async XLA Ops:
  2.7 0.8 copy-start
  3.5 0.8 copy-start.1
  4.2 0.8 copy-start.2
  5.0 0.8 copy-start.3
  58.2 29.4 %copy-start.7 = (f32[16,256]{1,0:T(8,128)S(1)}, f32[16,256]{1,0:T(8,128)}, u32[]{:S(2)}) copy-start(f32[16,256]{1,0:T(8,128)} %param.15) | copy-start | bytes 49156
  58.2 29.4 %copy-start.4 = (f32[16,4,2048]{2,1,0:T(4,128)S(1)}, f32[16,4,2048]{2,1,0:T(4,128)}, u32[]{:S(2)}) copy-start(f32[16,4,2048]{2,1,0:T(4,128)} %param.13) | copy-start | bytes 1572868
  58.3 29.4 %copy-start.5 = (f32[16,4,2048]{2,1,0:T(4,128)S(1)}, f32[16,4,2048]{2,1,0:T(4,128)}, u32[]{:S(2)}) copy-start(f32[16,4,2048]{2,1,0:T(4,128)} %param.14) | copy-start | bytes 1572868
  87.7 8.3 %copy-start.6 = (f32[16,256]{1,0:T(8,128)}, f32[16,256]{1,0:T(8,128)S(1)}, u32[]{:S(2)}) copy-start(f32[16,256]{1,0:T(8,128)S(1)} %fusion.18) | copy-start | bytes 49156

commit v2 on v1

--- a/solution.py
+++ b/solution.py
@@ -185,23 +185,77 @@
     lax.fori_loop(lo, hi, row, 0)
 
 
-def field_kernel(
-    source, observed, precision, conductivity, log_rows, grad_ref, info_ref,
+def project(fields, basis_rows, out):
+    count = fields.shape[0] // (RD * CH)
+    lane = lax.broadcasted_iota(jnp.int32, (CH, 256), 1) % RD
+    for q in range(4):
+        full = lax.dot_general(
+            fields[...], basis_rows[pl.ds(256 * q, 256), :], (((1,), (1,)), ((), ())),
+            preferred_element_type=F32,
+        )
+        for f in range(count):
+            rows = full[64 * f : 64 * f + 64]
+            part = rows[48:64]
+            for x in range(RD - 1):
+                part = jnp.where(lane == x, rows[16 * x : 16 * x + 16], part)
+            for h in range(2):
+                piece = part[:, 128 * h : 128 * h + 128]
+                if count == 1:
+                    out[2 * q + h] = piece
+                else:
+                    out[pl.ds(16 * (2 * q + h), 16), f, :] = piece
+
+
+def over_rows(value):
+    lane = lax.broadcasted_iota(jnp.int32, value.shape, 1)
+    pair = value + jnp.where(lane % 2 == 0, pltpu.roll(value, 127, 1), pltpu.roll(value, 1, 1))
+    return pair + jnp.where(lane % 4 < 2, pltpu.roll(pair, 126, 1), pltpu.roll(pair, 2, 1))
+
+
+def in_three(value):
+    high = value.astype(jnp.bfloat16)
+    rest = value - high.astype(F32)
+    middle = rest.astype(jnp.bfloat16)
+    low = (rest - middle.astype(F32)).astype(jnp.bfloat16)
+    return jnp.concatenate([high, middle, low], axis=0)
+
+
+def join_three(value, count):
+    return value[:count] + value[count : 2 * count] + value[2 * count : 3 * count]
+
+
+def step_kernel(
+    source, observed, precision, conductivity, log_field, noise_field, subspace, eigen, basis,
+    proposal, coef_ref, info_ref,
     lf, dinv, v, wu, wl, ws, sx, ox, px, state, cb, sb, ob, pb, mom_a, mom_b,
-    local_sem, send_sem, recv_sem, all_sem,
+    nf, bm, f2, fg, ps2, got2, sum2, ps, got, sums, wide_f, pick, em, pr,
+    local_sem, send_sem, recv_sem, all_sem, field_sem, out_sem,
 ):
     me = lax.axis_index(AXIS)
     own = [
-        pltpu.make_async_copy(log_rows, lf.at[pl.ds(RD, RD)], local_sem.at[0]),
         pltpu.make_async_copy(conductivity, cb.at[2], local_sem.at[1]),
         pltpu.make_async_copy(source, sb.at[1], local_sem.at[2]),
         pltpu.make_async_copy(observed, ob.at[1], local_sem.at[3]),
         pltpu.make_async_copy(precision, pb.at[1], local_sem.at[4]),
     ]
-    for copy in own:
+    logs = [
+        pltpu.make_async_copy(log_field.at[:, x, :], lf.at[RD + x], field_sem.at[x]) for x in range(RD)
+    ]
+    noises = [
+        pltpu.make_async_copy(noise_field.at[:, x, :], nf.at[x], field_sem.at[RD + x]) for x in range(RD)
+    ]
+    barrier = greet_all(me)
+    for copy in own + logs + noises:
         copy.start()
-    barrier = greet_all(me)
-    for copy in own:
+
+    def fetch(r, carry):
+        pltpu.make_async_copy(
+            basis.at[r], bm.at[pl.ds(pl.multiple_of(RD * r, RD), RD)], local_sem.at[0]
+        ).start()
+        return carry
+
+    lax.fori_loop(0, basis.shape[0], fetch, 0, unroll=8)
+    for copy in own + logs:
         copy.wait()
     pl.semaphore_wait(barrier, N - 1)
 
@@ -236,6 +290,15 @@
         late.append(remote(block.at[1], block.at[0], 1))
         late.append(remote(block.at[1], block.at[2], -1))
 
+    for x in range(RD):
+        f2[pl.ds(16 * x, 16), :] = lf[RD + x].astype(jnp.bfloat16)
+    for copy in noises:
+        copy.wait()
+    for x in range(RD):
+        f2[pl.ds(64 + 16 * x, 16), :] = nf[x].astype(jnp.bfloat16)
+    pltpu.make_async_copy(bm, bm, local_sem.at[0]).wait()
+    project(f2, bm, ps2)
+
     for copy in early:
         copy.wait()
 
@@ -284,6 +347,17 @@
         below.wait()
         start_row(RD - 1 - i, first)
         start_row(2 * RD + i, last)
+
+    def spread2(step, carry):
+        to = lax.rem(me + step, N)
+        pltpu.make_async_remote_copy(
+            src_ref=ps2.at[to], dst_ref=got2.at[me], send_sem=all_sem.at[4], recv_sem=all_sem.at[5],
+            device_id=(to,), device_id_type=MESH_ID,
+        ).start()
+        return carry
+
+    lax.fori_loop(1, N, spread2, 0, unroll=8)
+    got2[me] = ps2[me]
 
     def moments_zero(side):
         zero = jnp.zeros((8, 128), F32)
@@ -312,6 +386,29 @@
             powers_halo(v, k, wu, wl, dinv, lane, k + 1, RD)
     mom_a[me] = pack(accs)
     send_row_to_all(me, mom_a, all_sem.at[0], all_sem.at[1])
+
+    variance = 1.0 / (1.0 + eigen[...])
+    below = 2.0 + 0.8 * variance
+    factors = jnp.concatenate(
+        [
+            (2.0 - 0.8 * variance) / below,
+            1.6 * variance / below,
+            jnp.sqrt(6.4 * variance) / below,
+            jnp.zeros((5, variance.shape[1]), F32),
+            subspace[...],
+        ],
+        axis=0,
+    )
+    rank = factors.shape[1]
+    row_id = lax.broadcasted_iota(jnp.int32, (rank, RD * rank), 0)
+    lane_id = lax.broadcasted_iota(jnp.int32, (rank, RD * rank), 1)
+    widen = jnp.where(lane_id // RD == row_id, 1.0, 0.0).astype(jnp.bfloat16)
+    wide_f[...] = join_three(
+        jnp.dot(in_three(factors), widen, preferred_element_type=F32), 8 + CH
+    )
+    row_id = lax.broadcasted_iota(jnp.int32, (RD * rank, rank), 0)
+    lane_id = lax.broadcasted_iota(jnp.int32, (RD * rank, rank), 1)
+    pick[...] = jnp.where(row_id == RD * lane_id, 1.0, 0.0).astype(jnp.bfloat16)
 
     for copy in late:
         copy.wait()
@@ -330,6 +427,10 @@
     wait_rows(mom_a, all_sem.at[1])
     y, info = krylov_weights(unpack(jnp.sum(mom_a[...], axis=0)))
     info_ref[0] = jnp.broadcast_to(info, (CH, 128))
+
+    wait_rows(got2, all_sem.at[5])
+    sum2[me] = over_rows(jnp.sum(got2[...], axis=0))
+    send_row_to_all(me, sum2, all_sem.at[6], all_sem.at[7])
 
     def adjoint_start(e, carry):
         out = []
@@ -366,111 +467,111 @@
     y, info = krylov_weights(unpack(jnp.sum(mom_b[...], axis=0)))
     info_ref[1] = jnp.broadcast_to(info, (CH, 128))
 
-    def gradient(r, carry):
+    for r in range(RD):
         for h in range(4):
             sl = pl.ds(512 * h, 512)
             adj = y[0] * v[0, r + RD, :, sl]
             for k in range(1, ITERS):
                 adj = adj + y[k] * v[k, r + RD, :, sl]
             value = -jnp.exp(lf[r + RD, :, sl]) * adj * state[r + RD, :, sl]
-            grad_ref[r, :, sl] = value.astype(jnp.bfloat16)
-        return carry
-
-    lax.fori_loop(0, RD, gradient, 0)
-    wait_rows(mom_a, all_sem.at[0])
-    wait_rows(mom_b, all_sem.at[2])
-
-
-def solve_fields(source, observed, precision, conductivity, log_rows):
+            fg[pl.ds(16 * r, 16), sl] = value.astype(jnp.bfloat16)
+    project(fg, bm, ps)
+
+    def spread(step, carry):
+        to = lax.rem(me + step, N)
+        pltpu.make_async_remote_copy(
+            src_ref=ps.at[to // CH, pl.ds(to % CH, 1)], dst_ref=got.at[me],
+            send_sem=all_sem.at[8], recv_sem=all_sem.at[9],
+            device_id=(to,), device_id_type=MESH_ID,
+        ).start()
+        return carry
+
+    lax.fori_loop(1, N, spread, 0, unroll=8)
+    got[me] = ps[me // CH, pl.ds(me % CH, 1), :]
+    wait_rows(got, all_sem.at[9])
+    sums[me] = over_rows(jnp.sum(got[...], axis=0))
+    send_row_to_all(me, sums, all_sem.at[10], all_sem.at[11])
+    wait_rows(sum2, all_sem.at[7])
+    wait_rows(sums, all_sem.at[11])
+
+    lane = lax.broadcasted_iota(jnp.int32, (CH, 128), 1) % RD
+    pieces = []
+    for b in range(8):
+        rows = pl.ds(16 * b, 16)
+        cols = pl.ds(128 * b, 128)
+        state_coef, noise_coef = sum2[rows, 0, :], sum2[rows, 1, :]
+        new = wide_f[0:1, cols] * state_coef - wide_f[1:2, cols] * sums[rows, 0, :]
+        new = new + wide_f[2:3, cols] * wide_f[8 : 8 + CH, cols]
+        correction = new - 0.6 * state_coef - 0.8 * noise_coef
+        for x in range(RD):
+            em[pl.ds(16 * x, 16), cols] = jnp.where(lane == x, correction, 0.0).astype(jnp.bfloat16)
+        pieces.append(new)
+    for h in range(4):
+        sl = pl.ds(512 * h, 512)
+        rebuilt = jnp.dot(em[...], bm[:, sl], preferred_element_type=F32)
+        for x in range(RD):
+            pr[x, :, sl] = 0.6 * lf[RD + x, :, sl] + 0.8 * nf[x, :, sl] + rebuilt[16 * x : 16 * x + 16]
+    results = [pltpu.make_async_copy(pr.at[x], proposal.at[:, x, :], out_sem.at[x]) for x in range(RD)]
+    for copy in results:
+        copy.start()
+    coef_ref[...] = join_three(
+        jnp.dot(in_three(jnp.concatenate(pieces, axis=1)), pick[...], preferred_element_type=F32), CH
+    )
+    for buf, sem in ((mom_a, 0), (mom_b, 2), (got2, 4), (sum2, 6), (got, 8), (sums, 10)):
+        wait_rows(buf, all_sem.at[sem])
+    for copy in results:
+        copy.wait()
+
+
+def per_device(
+    source, observed, precision, conductivity, log_field, noise_field, subspace_noise, eigenvalues, basis,
+):
     any_space = pl.BlockSpec(memory_space=pl.ANY)
     vmem = pl.BlockSpec(memory_space=pltpu.VMEM)
+    rank = eigenvalues.shape[0]
     wide = pltpu.VMEM((EXT, CH, NY), F32)
     row8 = pltpu.VMEM((EXT, 8, NY), F32)
     small = pltpu.VMEM((3, RD, NY), F32)
-    return pl.pallas_call(
-        field_kernel,
+    one = pltpu.VMEM((N, 1, 128), F32)
+    two = pltpu.VMEM((N, 2, 128), F32)
+    half = jnp.bfloat16
+    proposal, new_coef, info = pl.pallas_call(
+        step_kernel,
         out_shape=(
-            jax.ShapeDtypeStruct((RD, CH, NY), jnp.bfloat16),
+            jax.ShapeDtypeStruct(log_field.shape, F32),
+            jax.ShapeDtypeStruct((CH, rank), F32),
             jax.ShapeDtypeStruct((2, CH, 128), F32),
         ),
-        in_specs=[any_space] * 5,
-        out_specs=(vmem, vmem),
+        in_specs=[any_space] * 6 + [vmem] * 2 + [any_space],
+        out_specs=(any_space, vmem, vmem),
         scratch_shapes=[
             wide, wide, pltpu.VMEM((ITERS, EXT, CH, NY), F32),
             pltpu.VMEM((EXT + 1, 8, NY), F32), row8, row8, row8, row8, row8, wide,
-            pltpu.VMEM((5, RD, NY), F32), small, small, small,
-            pltpu.VMEM((N, 1, 128), F32), pltpu.VMEM((N, 1, 128), F32),
+            pltpu.VMEM((5, RD, NY), F32), small, small, small, one, one,
+            pltpu.VMEM((RD, CH, NY), F32),
+            pltpu.VMEM((RD * rank, NY), half),
+            pltpu.VMEM((2 * RD * CH, NY), half),
+            pltpu.VMEM((RD * CH, NY), half),
+            two, two, two,
+            pltpu.VMEM((8, CH, 128), F32), one, one,
+            pltpu.VMEM((8 + CH, RD * rank), F32),
+            pltpu.VMEM((RD * rank, rank), half),
+            pltpu.VMEM((RD * CH, RD * rank), half),
+            pltpu.VMEM((RD, CH, NY), F32),
             pltpu.SemaphoreType.DMA((5,)),
             pltpu.SemaphoreType.DMA((24,)),
             pltpu.SemaphoreType.DMA((24,)),
+            pltpu.SemaphoreType.DMA((12,)),
+            pltpu.SemaphoreType.DMA((8,)),
             pltpu.SemaphoreType.DMA((4,)),
         ],
         compiler_params=pltpu.CompilerParams(
-            collective_id=0, has_side_effects=True, vmem_limit_bytes=40 << 20
+            collective_id=0, has_side_effects=True, vmem_limit_bytes=48 << 20
         ),
-    )(source, observed, precision, conductivity, log_rows)
-
-
-def sum_kernel(part, total, got, mine, sems):
-    me = lax.axis_index(AXIS)
-    barrier = greet_all(me)
-    pl.semaphore_wait(barrier, N - 1)
-
-    def send(step, carry):
-        to = lax.rem(me + step, N)
-        pltpu.make_async_remote_copy(
-            src_ref=part.at[to], dst_ref=got.at[me], send_sem=sems.at[0], recv_sem=sems.at[1],
-            device_id=(to,), device_id_type=MESH_ID,
-        ).start()
-        return carry
-
-    lax.fori_loop(1, N, send, 0, unroll=8)
-    got[me] = part[me]
-    wait_rows(got, sems.at[1])
-    mine[me] = jnp.sum(got[...], axis=0)
-    send_row_to_all(me, mine, sems.at[2], sems.at[3])
-    wait_rows(mine, sems.at[3])
-    total[...] = mine[...]
-    wait_rows(got, sems.at[0])
-    wait_rows(mine, sems.at[2])
-
-
-def sum_all(coefs):
-    flat = jnp.pad(coefs.reshape(N, 1, -1), ((0, 0), (0, 0), (0, 32)))
-    vmem = pl.BlockSpec(memory_space=pltpu.VMEM)
-    total = pl.pallas_call(
-        sum_kernel,
-        out_shape=jax.ShapeDtypeStruct((N, 1, 128), F32),
-        in_specs=[vmem],
-        out_specs=vmem,
-        scratch_shapes=[
-            pltpu.VMEM((N, 1, 128), F32), pltpu.VMEM((N, 1, 128), F32), pltpu.SemaphoreType.DMA((4,)),
-        ],
-        compiler_params=pltpu.CompilerParams(collective_id=1, has_side_effects=True),
-    )(flat)
-    return total[:, :, :96].reshape(coefs.shape)
-
-
-def per_device(
-    source, observed, precision, conductivity, log_field, noise_field, subspace_noise, eigenvalues, basis,
-):
-    log_rows = jnp.transpose(log_field, (1, 0, 2))
-    gradient, info = solve_fields(source, observed, precision, conductivity, log_rows)
-    gradient = jnp.transpose(gradient, (1, 0, 2))
-    stacked = jnp.concatenate(
-        [log_field.astype(jnp.bfloat16), noise_field.astype(jnp.bfloat16), gradient], 0
+    )(
+        source, observed, precision, conductivity, log_field, noise_field,
+        subspace_noise, eigenvalues.reshape(1, rank), basis,
     )
-    part = jnp.einsum("cxy,rxy->cr", stacked, basis, preferred_element_type=F32)
-    coefs = sum_all(part)
-    state_coef, noise_coef, grad_coef = coefs[:CH], coefs[CH : 2 * CH], coefs[2 * CH :]
-    variance = 1.0 / (1.0 + eigenvalues)
-    keep_factor = (2.0 - 0.8 * variance) / (2.0 + 0.8 * variance)
-    drift_factor = 1.6 * variance / (2.0 + 0.8 * variance)
-    noise_factor = jnp.sqrt(6.4 * variance) / (2.0 + 0.8 * variance)
-    new_coef = keep_factor * state_coef - drift_factor * grad_coef + noise_factor * subspace_noise
-    correction = (new_coef - 0.6 * state_coef - 0.8 * noise_coef).astype(jnp.bfloat16)
-    rebuilt = jnp.einsum("cr,rxy->cxy", correction, basis, preferred_element_type=F32)
-    proposal = 0.6 * log_field + 0.8 * noise_field + rebuilt
     return (proposal, new_coef)
 
 

time: 96.7 us -> 81.5 us (0.84)
  matrix products: 13.9 us -> 0 us
    dot_general x2 -> x0, matrix products: 13.9 us -> none  [the longest x1 7.15 us: per_device(): jnp.einsum('cr,rxy->cxy', correction, basis, preferred_element_type=F32)]
    unnamed x20, local copies, waits for them, and re-layouts: 8.29 us -> 10.1 us
    slice x1 -> x0, local copies, waits for them, and re-layouts: 1.02 us -> none  [sum_all(): return total[:, :, :96].reshape(coefs.shape)]
    pallas_call x2 -> x1, Pallas kernels: 70.5 us -> 70.1 us  [per_device(): pl.pallas_call(step_kernel, out_shape=(jax.ShapeDtypeStruct(log_field.sha...]
where the time goes in v2:
time: 81.5 us; the launch traced here: 80.9 us
  Pallas kernels  70.1 us (86%)
  local copies, waits for them, and re-layouts  10.1 us (12%)
    pallas_call x1, Pallas kernels, per_device(): pl.pallas_call(step_kernel, out_shape=(jax.ShapeDtypeStruct(log_field.sha...  70.1 us
    unnamed x20, local copies, waits for them, and re-layouts  10.1 us

profile of v2, /device:TPU:1, one launch (start us, length us, event | category | flops | bytes accessed | tf_op | source)
XLA Modules:
  0.0 80.9 jit_solution(1384488432892026089)
XLA Ops:
  0.6 0.0 copy-start
  0.6 2.2 %copy-done = bf16[256,4,2048]{2,1,0:T(4,128)(2,1)S(1)} copy-done((bf16[256,4,2048]{2,1,0:T(4,128)(2,1)S(1)}, bf16[256,4,2048]{2,1,0:T(4,128)(2,1)}, u32[]{:S(2)}) %copy-start) | copy-done | bytes 4194328
  2.8 0.0 copy-start.1
  2.8 1.0 %copy-done.1 = f32[16,4,2048]{2,1,0:T(4,128)S(1)} copy-done((f32[16,4,2048]{2,1,0:T(4,128)S(1)}, f32[16,4,2048]{2,1,0:T(4,128)}, u32[]{:S(2)}) %copy-start.1) | copy-done | bytes 524312
  3.9 0.0 copy-start.2
  3.9 1.0 %copy-done.2 = f32[16,4,2048]{2,1,0:T(4,128)S(1)} copy-done((f32[16,4,2048]{2,1,0:T(4,128)S(1)}, f32[16,4,2048]{2,1,0:T(4,128)}, u32[]{:S(2)}) %copy-start.2) | copy-done | bytes 524312
  4.9 0.0 copy-start.3
  4.9 0.8 copy-done.3
  5.7 0.0 copy-start.4
  5.7 0.8 copy-done.4
  6.4 0.0 copy-start.5
  6.4 0.8 copy-done.5
  7.2 0.0 copy-start.6
  7.2 0.8 copy-done.6
  7.9 0.0 copy-start.7
  7.9 0.7 copy-done.7
  8.7 0.0 copy-start.8
  8.7 0.7 copy-done.8
  9.3 70.1 %shard_map.104 = (f32[16,4,2048]{2,1,0:T(4,128)S(1)}, f32[16,256]{1,0:T(8,128)S(1)}, f32[2,16,128]{2,1,0:T(8,128)}) custom-call(f32[4,2048]{1,0:T(4,128)S(1)} %copy-done.3, f32[4,2048]{1,0:T(4,128)S(1)} %copy-done.4, f32[4,2048]{1,0:T(4,128)S(1)} %copy-done.5, f32[4,2048]{1,0:T(4,128)S(1)} %copy-done.6, f32[16,4,2048]{2,1,0:T(4,128)S(1)} %copy-done.1, ...), custom_call_target="tpu_custom_call" | custom-call | tf_op jit(solution)/shard_map/pallas_call | solution.py:538
  79.5 0.8 copy.13
  80.3 0.6 copy.14
Async XLA Ops:
  0.6 2.2 %copy-start = (bf16[256,4,2048]{2,1,0:T(4,128)(2,1)S(1)}, bf16[256,4,2048]{2,1,0:T(4,128)(2,1)}, u32[]{:S(2)}) copy-start(bf16[256,4,2048]{2,1,0:T(4,128)(2,1)} %basis.1) | copy-start | bytes 12582916
  2.8 1.0 %copy-start.1 = (f32[16,4,2048]{2,1,0:T(4,128)S(1)}, f32[16,4,2048]{2,1,0:T(4,128)}, u32[]{:S(2)}) copy-start(f32[16,4,2048]{2,1,0:T(4,128)} %log_field.1) | copy-start | bytes 1572868
  3.9 1.0 %copy-start.2 = (f32[16,4,2048]{2,1,0:T(4,128)S(1)}, f32[16,4,2048]{2,1,0:T(4,128)}, u32[]{:S(2)}) copy-start(f32[16,4,2048]{2,1,0:T(4,128)} %noise_field.1) | copy-start | bytes 1572868
  4.9 0.8 copy-start.3
  5.7 0.8 copy-start.4
  6.4 0.8 copy-start.5
  7.2 0.8 copy-start.6
  7.9 0.7 copy-start.7
  8.7 0.7 copy-start.8

commit v3 on v2

--- a/solution.py
+++ b/solution.py
@@ -225,10 +225,11 @@
 
 
 def step_kernel(
-    source, observed, precision, conductivity, log_field, noise_field, subspace, eigen, basis,
+    source, observed, precision, conductivity, log_field, noise_field, subspace_hbm, eigen_hbm, basis,
     proposal, coef_ref, info_ref,
     lf, dinv, v, wu, wl, ws, sx, ox, px, state, cb, sb, ob, pb, mom_a, mom_b,
     nf, bm, f2, fg, ps2, got2, sum2, ps, got, sums, wide_f, pick, em, pr,
+    subspace, eigen,
     local_sem, send_sem, recv_sem, all_sem, field_sem, out_sem,
 ):
     me = lax.axis_index(AXIS)
@@ -237,6 +238,8 @@
         pltpu.make_async_copy(source, sb.at[1], local_sem.at[2]),
         pltpu.make_async_copy(observed, ob.at[1], local_sem.at[3]),
         pltpu.make_async_copy(precision, pb.at[1], local_sem.at[4]),
+        pltpu.make_async_copy(subspace_hbm, subspace, local_sem.at[5]),
+        pltpu.make_async_copy(eigen_hbm, eigen, local_sem.at[6]),
     ]
     logs = [
         pltpu.make_async_copy(log_field.at[:, x, :], lf.at[RD + x], field_sem.at[x]) for x in range(RD)
@@ -526,7 +529,7 @@
 def per_device(
     source, observed, precision, conductivity, log_field, noise_field, subspace_noise, eigenvalues, basis,
 ):
-    any_space = pl.BlockSpec(memory_space=pl.ANY)
+    any_space = pl.BlockSpec(memory_space=pltpu.HBM)
     vmem = pl.BlockSpec(memory_space=pltpu.VMEM)
     rank = eigenvalues.shape[0]
     wide = pltpu.VMEM((EXT, CH, NY), F32)
@@ -542,7 +545,7 @@
             jax.ShapeDtypeStruct((CH, rank), F32),
             jax.ShapeDtypeStruct((2, CH, 128), F32),
         ),
-        in_specs=[any_space] * 6 + [vmem] * 2 + [any_space],
+        in_specs=[any_space] * 9,
         out_specs=(any_space, vmem, vmem),
         scratch_shapes=[
             wide, wide, pltpu.VMEM((ITERS, EXT, CH, NY), F32),
@@ -558,7 +561,8 @@
             pltpu.VMEM((RD * rank, rank), half),
             pltpu.VMEM((RD * CH, RD * rank), half),
             pltpu.VMEM((RD, CH, NY), F32),
-            pltpu.SemaphoreType.DMA((5,)),
+            pltpu.VMEM((CH, rank), F32), pltpu.VMEM((1, rank), F32),
+            pltpu.SemaphoreType.DMA((7,)),
             pltpu.SemaphoreType.DMA((24,)),
             pltpu.SemaphoreType.DMA((24,)),
             pltpu.SemaphoreType.DMA((12,)),
@@ -566,7 +570,7 @@
             pltpu.SemaphoreType.DMA((4,)),
         ],
         compiler_params=pltpu.CompilerParams(
-            collective_id=0, has_side_effects=True, vmem_limit_bytes=48 << 20
+            collective_id=0, has_side_effects=True, vmem_limit_bytes=66_900_000
         ),
     )(
         source, observed, precision, conductivity, log_field, noise_field,

time: 81.5 us -> 73.3 us (0.90)
  local copies, waits for them, and re-layouts: 10.1 us -> 3.21 us
  Pallas kernels: 70.1 us -> 69.2 us
    unnamed x20 -> x2, local copies, waits for them, and re-layouts: 10.1 us -> 3.21 us
    pallas_call x1, Pallas kernels: 70.1 us -> 69.2 us  [per_device(): pl.pallas_call(step_kernel, out_shape=(jax.ShapeDtypeStruct(log_field.sha...]
where the time goes in v3:
time: 73.3 us; the launch traced here: 73 us
  Pallas kernels  69.2 us (94%)
  local copies, waits for them, and re-layouts  3.21 us (4%)
    pallas_call x1, Pallas kernels, per_device(): pl.pallas_call(step_kernel, out_shape=(jax.ShapeDtypeStruct(log_field.sha...  69.2 us
    unnamed x2, local copies, waits for them, and re-layouts  3.21 us

profile of v3, /device:TPU:1, one launch (start us, length us, event | category | flops | bytes accessed | tf_op | source)
XLA Modules:
  0.0 73.0 jit_solution(6967211150909182419)
XLA Ops:
  0.6 69.2 %shard_map.104 = (f32[16,4,2048]{2,1,0:T(4,128)}, f32[16,256]{1,0:T(8,128)}, f32[2,16,128]{2,1,0:T(8,128)}) custom-call(f32[4,2048]{1,0:T(4,128)} %source.1, f32[4,2048]{1,0:T(4,128)} %observed.1, f32[4,2048]{1,0:T(4,128)} %precision.1, f32[4,2048]{1,0:T(4,128)} %conductivity.1, f32[16,4,2048]{2,1,0:T(4,128)} %log_field.1, f32[16,4,2048]{2,1,0:T(4,128)} %noise_field.1, ...), custom_call_target="tpu_custom_call" | custom-call | tf_op jit(solution)/shard_map/pallas_call | solution.py:541
  69.8 1.9 %copy.13 = f32[16,4,2048]{2,1,0:T(4,128)} copy(f32[16,4,2048]{2,1,0:T(4,128)} %get-tuple-element.8) | data formatting | bytes 1048576
  71.7 1.3 %copy.14 = f32[16,256]{1,0:T(8,128)} copy(f32[16,256]{1,0:T(8,128)} %get-tuple-element.9) | data formatting | bytes 32768

commit v4 on v3

--- a/solution.py
+++ b/solution.py
@@ -19,26 +19,44 @@
 F32 = jnp.float32
 
 
+def far_first(turn):
+    return lax.rem(2 + 3 * turn + 3 * (turn * (turn - 1) // 2), 4)
+
+
+def for_peers(me, act):
+    near = []
+    for z in (2, 1, 3, 0):
+        for c in (1, 0):
+            near.append(lax.rem(me + c, 2) + 2 * lax.rem(me // 2 + z, 4))
+
+    def plane(turn, carry):
+        y = lax.rem(me // 8 + far_first(lax.rem(turn, 4)), 4)
+        x = lax.rem(me // 32 + far_first(turn // 4), 4)
+        for at in near:
+            act(8 * y + 32 * x + at)
+        return carry
+
+    lax.fori_loop(0, 15, plane, 0)
+    for at in near[:-1]:
+        act(8 * (me // 8) + at)
+
+
 def greet_all(me):
     barrier = pltpu.get_barrier_semaphore()
-
-    def signal(step, carry):
-        pl.semaphore_signal(barrier, inc=1, device_id=(lax.rem(me + step, N),), device_id_type=MESH_ID)
-        return carry
-
-    lax.fori_loop(1, N, signal, 0)
+    for_peers(
+        me, lambda to: pl.semaphore_signal(barrier, inc=1, device_id=(to,), device_id_type=MESH_ID)
+    )
     return barrier
 
 
 def send_row_to_all(me, buf, send_sem, recv_sem):
-    def send(step, carry):
+    def send(to):
         pltpu.make_async_remote_copy(
             src_ref=buf.at[me], dst_ref=buf.at[me], send_sem=send_sem, recv_sem=recv_sem,
-            device_id=(lax.rem(me + step, N),), device_id_type=MESH_ID,
+            device_id=(to,), device_id_type=MESH_ID,
         ).start()
-        return carry
-
-    lax.fori_loop(1, N, send, 0, unroll=8)
+
+    for_peers(me, send)
 
 
 def wait_rows(buf, sem):
@@ -121,68 +139,67 @@
     return y, noise / gain
 
 
-def apply_row(vk, vn, wu, wl, dinv, e, g, lane, accs, store):
-    gs = pl.ds(8 * g, 8)
-
-    def tile(ref, row, j, rows=gs):
-        return ref[row, rows, pl.ds(128 * j, 128)]
-
+def apply_row(vk, vn, wu, wl, dinv, e, lane, accs):
     whole = pl.ds(0, 8)
-    v_at = {}
-    q_at = {}
-    r_at = {}
-    rq_at = {}
+    groups = (pl.ds(0, 8), pl.ds(8, 8))
+    kept = {}
 
     def prepare(j):
-        v = tile(vk, e, j)
-        w = tile(wl, e, j, whole)
-        v_at[j] = v
-        q_at[j] = w
-        r_at[j] = pltpu.roll(v, 1, 1)
-        rq_at[j] = pltpu.roll(w * v, 127, 1)
+        cols = pl.ds(128 * j, 128)
+        w = wl[e, whole, cols]
+        out = []
+        for gs in groups:
+            v = vk[e, gs, cols]
+            out.append((v, pltpu.roll(v, 1, 1), pltpu.roll(w * v, 127, 1)))
+        kept[j] = (w, out)
 
     prepare(0)
     for j in range(TILES):
+        cols = pl.ds(128 * j, 128)
         if j + 1 < TILES:
             prepare(j + 1)
-        left = r_at[j] if j == 0 else jnp.where(lane == 0, r_at[j - 1], r_at[j])
-        right = jnp.where(lane == 127, rq_at[j + 1] if j + 1 < TILES else 0.0, rq_at[j])
-        t = tile(wu, e, j, whole) * tile(vk, e - 1, j) + tile(wu, e + 1, j, whole) * tile(vk, e + 1, j)
-        t = t + (q_at[j] * left + right)
-        v = v_at[j]
-        if accs is not None:
-            accs = (accs[0] + t * v, accs[1])
-        if store:
-            new = t * tile(dinv, e, j)
-            vn[e, gs, pl.ds(128 * j, 128)] = new
+        w, here = kept[j]
+        above, below = wu[e, whole, cols], wu[e + 1, whole, cols]
+        for g, gs in enumerate(groups):
+            v, moved, moved_back = here[g]
+            left = moved if j == 0 else jnp.where(lane == 0, kept[j - 1][1][g][1], moved)
+            right = jnp.where(lane == 127, kept[j + 1][1][g][2] if j + 1 < TILES else 0.0, moved_back)
+            t = above * vk[e - 1, gs, cols] + below * vk[e + 1, gs, cols]
+            t = t + (w * left + right)
             if accs is not None:
-                accs = (accs[0], accs[1] + t * new)
-    return accs
+                accs[0][g] = accs[0][g] + t * v
+            if vn is not None:
+                new = t * dinv[e, gs, cols]
+                vn[e, gs, cols] = new
+                if accs is not None:
+                    accs[1][g] = accs[1][g] + t * new
 
 
 def powers_own(v, k, wu, wl, dinv, lane):
     zero = jnp.zeros((8, 128), F32)
-    store = k < ITERS - 1
-    vk = v.at[k]
-    vn = v.at[k + 1] if store else None
-
-    def row(e, carry):
-        return tuple(apply_row(vk, vn, wu, wl, dinv, e, g, lane, carry[g], store) for g in range(2))
-
-    got = lax.fori_loop(RD, 2 * RD, row, ((zero, zero), (zero, zero)))
-    return [got[0][0], got[1][0]], [got[0][1], got[1][1]]
-
-
-def powers_halo(v, k, wu, wl, dinv, lane, lo, hi):
-    vk, vn = v.at[k], v.at[k + 1]
-
-    def row(i, carry):
-        for e in (i, EXT - 1 - i):
-            for g in range(2):
-                apply_row(vk, vn, wu, wl, dinv, e, g, lane, None, True)
+
+    def rows(i, carry):
+        accs = [list(carry[0]), list(carry[1])]
+        for h in range(2):
+            e = RD + 2 * i + h
+            apply_row(v.at[k], v.at[k + 1] if k < ITERS - 1 else None, wu, wl, dinv, e, lane, accs)
+        return tuple(accs[0]), tuple(accs[1])
+
+    got = lax.fori_loop(0, RD // 2, rows, ((zero, zero), (zero, zero)))
+    return list(got[0]), list(got[1])
+
+
+def powers_pairs(v, wu, wl, dinv, lane, count, which):
+    def rows(step, carry):
+        k, i = which(step)
+        for e in (RD - i, 2 * RD - 1 + i):
+            apply_row(v.at[k], v.at[k + 1], wu, wl, dinv, e, lane, None)
         return carry
 
-    lax.fori_loop(lo, hi, row, 0)
+    if count == 1:
+        rows(0, 0)
+    else:
+        lax.fori_loop(0, count, rows, 0)
 
 
 def project(fields, basis_rows, out):
@@ -345,22 +362,6 @@
         return carry
 
     lax.fori_loop(RD, 2 * RD, own_start, 0)
-    for i, (above, below) in enumerate(rows):
-        above.wait()
-        below.wait()
-        start_row(RD - 1 - i, first)
-        start_row(2 * RD + i, last)
-
-    def spread2(step, carry):
-        to = lax.rem(me + step, N)
-        pltpu.make_async_remote_copy(
-            src_ref=ps2.at[to], dst_ref=got2.at[me], send_sem=all_sem.at[4], recv_sem=all_sem.at[5],
-            device_id=(to,), device_id_type=MESH_ID,
-        ).start()
-        return carry
-
-    lax.fori_loop(1, N, spread2, 0, unroll=8)
-    got2[me] = ps2[me]
 
     def moments_zero(side):
         zero = jnp.zeros((8, 128), F32)
@@ -379,16 +380,30 @@
 
     accs = [moments_zero(lambda e, g, sl: sx[e, :, sl])]
     moved = []
-    for k in range(ITERS):
-        one, two = powers_own(v, k, wu, wl, dinv, lane)
+    for i, (above, below) in enumerate(rows):
+        above.wait()
+        below.wait()
+        start_row(RD - 1 - i, first)
+        start_row(2 * RD + i, last)
+        if i > 0:
+            powers_pairs(v, wu, wl, dinv, lane, i, lambda k: (k, i - k))
+        one, two = powers_own(v, i, wu, wl, dinv, lane)
         accs.append(one)
-        if k < ITERS - 1:
+        if i < ITERS - 1:
             accs.append(two)
-            moved.append(remote(v.at[k + 1, RD], v.at[k + 1, 0], 1))
-            moved.append(remote(v.at[k + 1, 2 * RD - 1], v.at[k + 1, EXT - 1], -1))
-            powers_halo(v, k, wu, wl, dinv, lane, k + 1, RD)
+            moved.append(remote(v.at[i + 1, RD], v.at[i + 1, 0], 1))
+            moved.append(remote(v.at[i + 1, 2 * RD - 1], v.at[i + 1, EXT - 1], -1))
     mom_a[me] = pack(accs)
     send_row_to_all(me, mom_a, all_sem.at[0], all_sem.at[1])
+
+    def spread2(to):
+        pltpu.make_async_remote_copy(
+            src_ref=ps2.at[to], dst_ref=got2.at[me], send_sem=all_sem.at[4], recv_sem=all_sem.at[5],
+            device_id=(to,), device_id_type=MESH_ID,
+        ).start()
+    for_peers(me, spread2)
+    got2[me] = ps2[me]
+
 
     variance = 1.0 / (1.0 + eigen[...])
     below = 2.0 + 0.8 * variance
@@ -420,10 +435,10 @@
         px[e] = jnp.broadcast_to(pb[e // RD, pl.ds(e % RD, 1), :], (8, NY))
     moved[0].wait()
     moved[1].wait()
-    powers_halo(v, 1, wu, wl, dinv, lane, 1, 2)
+    powers_pairs(v, wu, wl, dinv, lane, 1, lambda step: (1, 3))
     moved[2].wait()
     moved[3].wait()
-    powers_halo(v, 2, wu, wl, dinv, lane, 1, 3)
+    powers_pairs(v, wu, wl, dinv, lane, 2, lambda step: (2, 2 + step))
     moved[4].wait()
     moved[5].wait()
 
@@ -463,7 +478,7 @@
         accs.append(one)
         if k < ITERS - 1:
             accs.append(two)
-            powers_halo(v, k, wu, wl, dinv, lane, k + 1, RD)
+            powers_pairs(v, wu, wl, dinv, lane, RD - 1 - k, lambda step: (k, 1 + step))
     mom_b[me] = pack(accs)
     send_row_to_all(me, mom_b, all_sem.at[2], all_sem.at[3])
     wait_rows(mom_b, all_sem.at[3])
@@ -480,16 +495,13 @@
             fg[pl.ds(16 * r, 16), sl] = value.astype(jnp.bfloat16)
     project(fg, bm, ps)
 
-    def spread(step, carry):
-        to = lax.rem(me + step, N)
+    def spread(to):
         pltpu.make_async_remote_copy(
             src_ref=ps.at[to // CH, pl.ds(to % CH, 1)], dst_ref=got.at[me],
             send_sem=all_sem.at[8], recv_sem=all_sem.at[9],
             device_id=(to,), device_id_type=MESH_ID,
         ).start()
-        return carry
-
-    lax.fori_loop(1, N, spread, 0, unroll=8)
+    for_peers(me, spread)
     got[me] = ps[me // CH, pl.ds(me % CH, 1), :]
     wait_rows(got, all_sem.at[9])
     sums[me] = over_rows(jnp.sum(got[...], axis=0))

time: 73.3 us -> 64 us (0.87)
  Pallas kernels: 69.2 us -> 59.9 us
    pallas_call x1, Pallas kernels: 69.2 us -> 59.9 us  [per_device(): pl.pallas_call(step_kernel, out_shape=(jax.ShapeDtypeStruct(log_field.sha...]
where the time goes in v4:
time: 64 us; the launch traced here: 63.7 us
  Pallas kernels  59.9 us (94%)
  local copies, waits for them, and re-layouts  3.21 us (5%)
  between operations  0.64 us (1%)
    pallas_call x1, Pallas kernels, per_device(): pl.pallas_call(step_kernel, out_shape=(jax.ShapeDtypeStruct(log_field.sha...  59.9 us
    unnamed x2, local copies, waits for them, and re-layouts  3.21 us

profile of v4, /device:TPU:1, one launch (start us, length us, event | category | flops | bytes accessed | tf_op | source)
XLA Modules:
  0.0 63.7 jit_solution(16902951923387259943)
XLA Ops:
  0.6 59.9 %shard_map.104 = (f32[16,4,2048]{2,1,0:T(4,128)}, f32[16,256]{1,0:T(8,128)}, f32[2,16,128]{2,1,0:T(8,128)}) custom-call(f32[4,2048]{1,0:T(4,128)} %source.1, f32[4,2048]{1,0:T(4,128)} %observed.1, f32[4,2048]{1,0:T(4,128)} %precision.1, f32[4,2048]{1,0:T(4,128)} %conductivity.1, f32[16,4,2048]{2,1,0:T(4,128)} %log_field.1, f32[16,4,2048]{2,1,0:T(4,128)} %noise_field.1, ...), custom_call_target="tpu_custom_call" | custom-call | tf_op jit(solution)/shard_map/pallas_call | solution.py:553
  60.5 1.9 %copy.13 = f32[16,4,2048]{2,1,0:T(4,128)} copy(f32[16,4,2048]{2,1,0:T(4,128)} %get-tuple-element.8) | data formatting | bytes 1048576
  62.4 1.3 %copy.14 = f32[16,256]{1,0:T(8,128)} copy(f32[16,256]{1,0:T(8,128)} %get-tuple-element.9) | data formatting | bytes 32768

commit v5 on v4

--- a/solution.py
+++ b/solution.py
@@ -41,12 +41,25 @@
         act(8 * (me // 8) + at)
 
 
-def greet_all(me):
+def ring_peers(me, stride):
+    at = lax.rem(me // stride, 4)
+    return [me + stride * (lax.rem(at + d, 4) - at) for d in (2, 1, 3)]
+
+
+def greet_near(me):
+    column = 8 * (me // 8)
+    near = [column + lax.rem(me + d, 8) for d in range(1, 8)]
+    near += ring_peers(me, 8) + ring_peers(me, 32)
+    near += [lax.rem(me + d + N, N) for d in (-2, 2, -1, 1)]
     barrier = pltpu.get_barrier_semaphore()
-    for_peers(
-        me, lambda to: pl.semaphore_signal(barrier, inc=1, device_id=(to,), device_id_type=MESH_ID)
-    )
-    return barrier
+    for to in near:
+        pl.semaphore_signal(barrier, inc=1, device_id=(to,), device_id_type=MESH_ID)
+    return barrier, len(near)
+
+
+def pass_on(me, sem, stride):
+    for to in ring_peers(me, stride):
+        pl.semaphore_signal(sem, inc=1, device_id=(to,), device_id_type=MESH_ID)
 
 
 def send_row_to_all(me, buf, send_sem, recv_sem):
@@ -182,24 +195,16 @@
         accs = [list(carry[0]), list(carry[1])]
         for h in range(2):
             e = RD + 2 * i + h
-            apply_row(v.at[k], v.at[k + 1] if k < ITERS - 1 else None, wu, wl, dinv, e, lane, accs)
+            apply_row(v[k], v[k + 1] if k < ITERS - 1 else None, wu, wl, dinv, e, lane, accs)
         return tuple(accs[0]), tuple(accs[1])
 
     got = lax.fori_loop(0, RD // 2, rows, ((zero, zero), (zero, zero)))
     return list(got[0]), list(got[1])
 
 
-def powers_pairs(v, wu, wl, dinv, lane, count, which):
-    def rows(step, carry):
-        k, i = which(step)
-        for e in (RD - i, 2 * RD - 1 + i):
-            apply_row(v.at[k], v.at[k + 1], wu, wl, dinv, e, lane, None)
-        return carry
-
-    if count == 1:
-        rows(0, 0)
-    else:
-        lax.fori_loop(0, count, rows, 0)
+def powers_pair(v, k, wu, wl, dinv, lane, i):
+    for e in (RD - i, 2 * RD - 1 + i):
+        apply_row(v[k], v[k + 1], wu, wl, dinv, e, lane, None)
 
 
 def project(fields, basis_rows, out):
@@ -244,12 +249,13 @@
 def step_kernel(
     source, observed, precision, conductivity, log_field, noise_field, subspace_hbm, eigen_hbm, basis,
     proposal, coef_ref, info_ref,
-    lf, dinv, v, wu, wl, ws, sx, ox, px, state, cb, sb, ob, pb, mom_a, mom_b,
+    lf, dinv, v0, v1, v2, v3, wu, wl, ws, sx, ox, px, state, cb, sb, ob, pb, mom_a, mom_b,
     nf, bm, f2, fg, ps2, got2, sum2, ps, got, sums, wide_f, pick, em, pr,
     subspace, eigen,
-    local_sem, send_sem, recv_sem, all_sem, field_sem, out_sem,
+    local_sem, send_sem, recv_sem, all_sem, field_sem, out_sem, ring_sem,
 ):
     me = lax.axis_index(AXIS)
+    v = (v0, v1, v2, v3)
     own = [
         pltpu.make_async_copy(conductivity, cb.at[2], local_sem.at[1]),
         pltpu.make_async_copy(source, sb.at[1], local_sem.at[2]),
@@ -264,7 +270,7 @@
     noises = [
         pltpu.make_async_copy(noise_field.at[:, x, :], nf.at[x], field_sem.at[RD + x]) for x in range(RD)
     ]
-    barrier = greet_all(me)
+    barrier, greeted = greet_near(me)
     for copy in own + logs + noises:
         copy.start()
 
@@ -277,7 +283,8 @@
     lax.fori_loop(0, basis.shape[0], fetch, 0, unroll=8)
     for copy in own + logs:
         copy.wait()
-    pl.semaphore_wait(barrier, N - 1)
+    pl.semaphore_wait(barrier, greeted)
+    pass_on(me, ring_sem.at[0], 8)
 
     count = [0]
 
@@ -318,6 +325,8 @@
         f2[pl.ds(64 + 16 * x, 16), :] = nf[x].astype(jnp.bfloat16)
     pltpu.make_async_copy(bm, bm, local_sem.at[0]).wait()
     project(f2, bm, ps2)
+    pl.semaphore_wait(ring_sem.at[0], 3)
+    pass_on(me, ring_sem.at[1], 32)
 
     for copy in early:
         copy.wait()
@@ -355,7 +364,7 @@
             gs = pl.ds(8 * g, 8)
             d = keep / (ws[e] + jnp.exp(lf[e, gs, :]))
             dinv[e, gs, :] = d
-            v[0, e, gs, :] = sx[e] * d
+            v0[e, gs, :] = sx[e] * d
 
     def own_start(e, carry):
         start_row(e, jnp.float32(1.0))
@@ -372,7 +381,7 @@
                 acc = carry[g]
                 for j in range(TILES):
                     sl = pl.ds(128 * j, 128)
-                    acc = acc + side(e, g, sl) * v[0, e, pl.ds(8 * g, 8), sl]
+                    acc = acc + side(e, g, sl) * v0[e, pl.ds(8 * g, 8), sl]
                 out.append(acc)
             return tuple(out)
 
@@ -385,16 +394,69 @@
         below.wait()
         start_row(RD - 1 - i, first)
         start_row(2 * RD + i, last)
-        if i > 0:
-            powers_pairs(v, wu, wl, dinv, lane, i, lambda k: (k, i - k))
+        for k in range(i):
+            powers_pair(v, k, wu, wl, dinv, lane, i - k)
         one, two = powers_own(v, i, wu, wl, dinv, lane)
         accs.append(one)
         if i < ITERS - 1:
             accs.append(two)
-            moved.append(remote(v.at[i + 1, RD], v.at[i + 1, 0], 1))
-            moved.append(remote(v.at[i + 1, 2 * RD - 1], v.at[i + 1, EXT - 1], -1))
+            moved.append(remote(v[i + 1].at[RD], v[i + 1].at[0], 1))
+            moved.append(remote(v[i + 1].at[2 * RD - 1], v[i + 1].at[EXT - 1], -1))
     mom_a[me] = pack(accs)
+    pl.semaphore_wait(ring_sem.at[1], 3)
     send_row_to_all(me, mom_a, all_sem.at[0], all_sem.at[1])
+
+    for copy in late:
+        copy.wait()
+    for e in range(EXT):
+        ox[e] = jnp.broadcast_to(ob[e // RD, pl.ds(e % RD, 1), :], (8, NY))
+        px[e] = jnp.broadcast_to(pb[e // RD, pl.ds(e % RD, 1), :], (8, NY))
+    moved[0].wait()
+    moved[1].wait()
+    powers_pair(v, 1, wu, wl, dinv, lane, 3)
+    moved[2].wait()
+    moved[3].wait()
+    powers_pair(v, 2, wu, wl, dinv, lane, 2)
+    powers_pair(v, 2, wu, wl, dinv, lane, 3)
+    moved[4].wait()
+    moved[5].wait()
+
+    wait_rows(mom_a, all_sem.at[1])
+    y, info = krylov_weights(unpack(jnp.sum(mom_a[...], axis=0)))
+    info_ref[0] = jnp.broadcast_to(info, (CH, 128))
+
+    def adjoint_start(e, carry):
+        out = []
+        for g in range(2):
+            acc = carry[g]
+            gs = pl.ds(8 * g, 8)
+            yg = [jnp.broadcast_to(y[k][8 * g:8 * g + 8], (8, 128)) for k in range(ITERS)]
+            for j in range(TILES):
+                sl = pl.ds(128 * j, 128)
+                x = yg[0] * v0[e, gs, sl]
+                for k in range(1, ITERS):
+                    x = x + yg[k] * v[k][e, gs, sl]
+                side = px[e, :, sl] * (x - ox[e, :, sl])
+                new = side * dinv[e, gs, sl]
+                state[e, gs, sl] = x
+                v0[e, gs, sl] = new
+                acc = acc + side * new
+            out.append(acc)
+        return tuple(out)
+
+    zero = jnp.zeros((8, 128), F32)
+    lax.fori_loop(0, RD, adjoint_start, (zero, zero))
+    lax.fori_loop(2 * RD, EXT, adjoint_start, (zero, zero))
+    accs = [list(lax.fori_loop(RD, 2 * RD, adjoint_start, (zero, zero)))]
+    for k in range(ITERS):
+        one, two = powers_own(v, k, wu, wl, dinv, lane)
+        accs.append(one)
+        if k < ITERS - 1:
+            accs.append(two)
+            for i in range(1, RD - k):
+                powers_pair(v, k, wu, wl, dinv, lane, i)
+    mom_b[me] = pack(accs)
+    send_row_to_all(me, mom_b, all_sem.at[2], all_sem.at[3])
 
     def spread2(to):
         pltpu.make_async_remote_copy(
@@ -428,59 +490,6 @@
     lane_id = lax.broadcasted_iota(jnp.int32, (RD * rank, rank), 1)
     pick[...] = jnp.where(row_id == RD * lane_id, 1.0, 0.0).astype(jnp.bfloat16)
 
-    for copy in late:
-        copy.wait()
-    for e in range(EXT):
-        ox[e] = jnp.broadcast_to(ob[e // RD, pl.ds(e % RD, 1), :], (8, NY))
-        px[e] = jnp.broadcast_to(pb[e // RD, pl.ds(e % RD, 1), :], (8, NY))
-    moved[0].wait()
-    moved[1].wait()
-    powers_pairs(v, wu, wl, dinv, lane, 1, lambda step: (1, 3))
-    moved[2].wait()
-    moved[3].wait()
-    powers_pairs(v, wu, wl, dinv, lane, 2, lambda step: (2, 2 + step))
-    moved[4].wait()
-    moved[5].wait()
-
-    wait_rows(mom_a, all_sem.at[1])
-    y, info = krylov_weights(unpack(jnp.sum(mom_a[...], axis=0)))
-    info_ref[0] = jnp.broadcast_to(info, (CH, 128))
-
-    wait_rows(got2, all_sem.at[5])
-    sum2[me] = over_rows(jnp.sum(got2[...], axis=0))
-    send_row_to_all(me, sum2, all_sem.at[6], all_sem.at[7])
-
-    def adjoint_start(e, carry):
-        out = []
-        for g in range(2):
-            acc = carry[g]
-            gs = pl.ds(8 * g, 8)
-            yg = [jnp.broadcast_to(y[k][8 * g:8 * g + 8], (8, 128)) for k in range(ITERS)]
-            for j in range(TILES):
-                sl = pl.ds(128 * j, 128)
-                x = yg[0] * v[0, e, gs, sl]
-                for k in range(1, ITERS):
-                    x = x + yg[k] * v[k, e, gs, sl]
-                side = px[e, :, sl] * (x - ox[e, :, sl])
-                new = side * dinv[e, gs, sl]
-                state[e, gs, sl] = x
-                v[0, e, gs, sl] = new
-                acc = acc + side * new
-            out.append(acc)
-        return tuple(out)
-
-    zero = jnp.zeros((8, 128), F32)
-    lax.fori_loop(0, RD, adjoint_start, (zero, zero))
-    lax.fori_loop(2 * RD, EXT, adjoint_start, (zero, zero))
-    accs = [list(lax.fori_loop(RD, 2 * RD, adjoint_start, (zero, zero)))]
-    for k in range(ITERS):
-        one, two = powers_own(v, k, wu, wl, dinv, lane)
-        accs.append(one)
-        if k < ITERS - 1:
-            accs.append(two)
-            powers_pairs(v, wu, wl, dinv, lane, RD - 1 - k, lambda step: (k, 1 + step))
-    mom_b[me] = pack(accs)
-    send_row_to_all(me, mom_b, all_sem.at[2], all_sem.at[3])
     wait_rows(mom_b, all_sem.at[3])
     y, info = krylov_weights(unpack(jnp.sum(mom_b[...], axis=0)))
     info_ref[1] = jnp.broadcast_to(info, (CH, 128))
@@ -488,9 +497,9 @@
     for r in range(RD):
         for h in range(4):
             sl = pl.ds(512 * h, 512)
-            adj = y[0] * v[0, r + RD, :, sl]
+            adj = y[0] * v0[r + RD, :, sl]
             for k in range(1, ITERS):
-                adj = adj + y[k] * v[k, r + RD, :, sl]
+                adj = adj + y[k] * v[k][r + RD, :, sl]
             value = -jnp.exp(lf[r + RD, :, sl]) * adj * state[r + RD, :, sl]
             fg[pl.ds(16 * r, 16), sl] = value.astype(jnp.bfloat16)
     project(fg, bm, ps)
@@ -503,6 +512,10 @@
         ).start()
     for_peers(me, spread)
     got[me] = ps[me // CH, pl.ds(me % CH, 1), :]
+    wait_rows(got2, all_sem.at[5])
+    sum2[me] = over_rows(jnp.sum(got2[...], axis=0))
+    send_row_to_all(me, sum2, all_sem.at[6], all_sem.at[7])
+
     wait_rows(got, all_sem.at[9])
     sums[me] = over_rows(jnp.sum(got[...], axis=0))
     send_row_to_all(me, sums, all_sem.at[10], all_sem.at[11])
@@ -560,7 +573,7 @@
         in_specs=[any_space] * 9,
         out_specs=(any_space, vmem, vmem),
         scratch_shapes=[
-            wide, wide, pltpu.VMEM((ITERS, EXT, CH, NY), F32),
+            wide, wide, wide, wide, wide, wide,
             pltpu.VMEM((EXT + 1, 8, NY), F32), row8, row8, row8, row8, row8, wide,
             pltpu.VMEM((5, RD, NY), F32), small, small, small, one, one,
             pltpu.VMEM((RD, CH, NY), F32),
@@ -580,6 +593,7 @@
             pltpu.SemaphoreType.DMA((12,)),
             pltpu.SemaphoreType.DMA((8,)),
             pltpu.SemaphoreType.DMA((4,)),
+            pltpu.SemaphoreType.REGULAR((2,)),
         ],
         compiler_params=pltpu.CompilerParams(
             collective_id=0, has_side_effects=True, vmem_limit_bytes=66_900_000

time: 64 us -> 59.8 us (0.934)
  Pallas kernels: 59.9 us -> 55.7 us
    pallas_call x1, Pallas kernels: 59.9 us -> 55.7 us  [per_device(): pl.pallas_call(step_kernel, out_shape=(jax.ShapeDtypeStruct(log_field.sha...]
where the time goes in v5:
time: 59.8 us; the launch traced here: 59.5 us
  Pallas kernels  55.7 us (93%)
  local copies, waits for them, and re-layouts  3.21 us (5%)
  between operations  0.64 us (1%)
    pallas_call x1, Pallas kernels, per_device(): pl.pallas_call(step_kernel, out_shape=(jax.ShapeDtypeStruct(log_field.sha...  55.7 us
    unnamed x2, local copies, waits for them, and re-layouts  3.21 us

profile of v5, /device:TPU:1, one launch (start us, length us, event | category | flops | bytes accessed | tf_op | source)
XLA Modules:
  0.0 59.5 jit_solution(5960499228736690195)
XLA Ops:
  0.6 55.7 %shard_map.104 = (f32[16,4,2048]{2,1,0:T(4,128)}, f32[16,256]{1,0:T(8,128)}, f32[2,16,128]{2,1,0:T(8,128)}) custom-call(f32[4,2048]{1,0:T(4,128)} %source.1, f32[4,2048]{1,0:T(4,128)} %observed.1, f32[4,2048]{1,0:T(4,128)} %precision.1, f32[4,2048]{1,0:T(4,128)} %conductivity.1, f32[16,4,2048]{2,1,0:T(4,128)} %log_field.1, f32[16,4,2048]{2,1,0:T(4,128)} %noise_field.1, ...), custom_call_target="tpu_custom_call" | custom-call | tf_op jit(solution)/shard_map/pallas_call | solution.py:566
  56.3 1.9 %copy.13 = f32[16,4,2048]{2,1,0:T(4,128)} copy(f32[16,4,2048]{2,1,0:T(4,128)} %get-tuple-element.8) | data formatting | bytes 1048576
  58.2 1.3 %copy.14 = f32[16,256]{1,0:T(8,128)} copy(f32[16,256]{1,0:T(8,128)} %get-tuple-element.9) | data formatting | bytes 32768

commit v6 on v5

--- a/solution.py
+++ b/solution.py
@@ -246,6 +246,17 @@
     return value[:count] + value[count : 2 * count] + value[2 * count : 3 * count]
 
 
+def empty_side(row, end, lf, cb, sb, ob, pb, v):
+    block = row // RD
+    lf[pl.ds(row, RD)] = jnp.zeros((RD, CH, NY), F32)
+    for at in (0, 1):
+        cb[(0 if row == 0 else 3) + at] = jnp.zeros((RD, NY), F32)
+    for small in (sb, ob, pb):
+        small[block] = jnp.zeros((RD, NY), F32)
+    for power in v[1:]:
+        power[end] = jnp.zeros((CH, NY), F32)
+
+
 def step_kernel(
     source, observed, precision, conductivity, log_field, noise_field, subspace_hbm, eigen_hbm, basis,
     proposal, coef_ref, info_ref,
@@ -271,22 +282,16 @@
         pltpu.make_async_copy(noise_field.at[:, x, :], nf.at[x], field_sem.at[RD + x]) for x in range(RD)
     ]
     barrier, greeted = greet_near(me)
-    for copy in own + logs + noises:
+    for copy in own + logs:
         copy.start()
 
-    def fetch(r, carry):
-        pltpu.make_async_copy(
-            basis.at[r], bm.at[pl.ds(pl.multiple_of(RD * r, RD), RD)], local_sem.at[0]
-        ).start()
-        return carry
-
-    lax.fori_loop(0, basis.shape[0], fetch, 0, unroll=8)
     for copy in own + logs:
         copy.wait()
     pl.semaphore_wait(barrier, greeted)
     pass_on(me, ring_sem.at[0], 8)
 
     count = [0]
+    sent = []
 
     def remote(src, dst, shift):
         index = count[0]
@@ -295,8 +300,38 @@
             src_ref=src, dst_ref=dst, send_sem=send_sem.at[index], recv_sem=recv_sem.at[index],
             device_id=(lax.rem(me + shift + N, N),), device_id_type=MESH_ID,
         )
-        copy.start()
-        return copy
+        goes = me + shift < N if shift > 0 else me + shift >= 0
+        comes = me - shift >= 0 if shift > 0 else me - shift < N
+
+        @pl.when(goes)
+        def _():
+            copy.start()
+
+        sent.append((copy, goes))
+        return copy, comes
+
+    def arrived(*pairs):
+        for copy, comes in pairs:
+
+            @pl.when(comes)
+            def _():
+                copy.wait_recv()
+
+    @pl.when(me == 0)
+    def _():
+        empty_side(0, 0, lf, cb, sb, ob, pb, v)
+
+    @pl.when(me == N - 1)
+    def _():
+        empty_side(2 * RD, EXT - 1, lf, cb, sb, ob, pb, v)
+
+    @pl.when(me == 1)
+    def _():
+        cb[0] = jnp.zeros((RD, NY), F32)
+
+    @pl.when(me == N - 2)
+    def _():
+        cb[4] = jnp.zeros((RD, NY), F32)
 
     early = []
     for block, src, centre in ((cb, 2, 2), (sb, 1, 1)):
@@ -317,6 +352,16 @@
         late.append(remote(block.at[1], block.at[0], 1))
         late.append(remote(block.at[1], block.at[2], -1))
 
+    for copy in noises:
+        copy.start()
+
+    def fetch(r, carry):
+        pltpu.make_async_copy(
+            basis.at[r], bm.at[pl.ds(pl.multiple_of(RD * r, RD), RD)], local_sem.at[0]
+        ).start()
+        return carry
+
+    lax.fori_loop(0, basis.shape[0], fetch, 0, unroll=8)
     for x in range(RD):
         f2[pl.ds(16 * x, 16), :] = lf[RD + x].astype(jnp.bfloat16)
     for copy in noises:
@@ -328,8 +373,7 @@
     pl.semaphore_wait(ring_sem.at[0], 3)
     pass_on(me, ring_sem.at[1], 32)
 
-    for copy in early:
-        copy.wait()
+    arrived(*early)
 
     lane = lax.broadcasted_iota(jnp.int32, (8, 128), 1)
     first = jnp.where(me == 0, 0.0, 1.0).astype(F32)
@@ -345,6 +389,10 @@
             a = first * a + (1.0 - first) * b
         if e == 2 * RD:
             b = last * b + (1.0 - last) * a
+        if e == 0:
+            a = jnp.where(me == 1, b, a)
+        if e == EXT:
+            b = jnp.where(me == N - 2, a, b)
         return 0.5 * (a + b)
 
     for e in range(EXT + 1):
@@ -390,8 +438,7 @@
     accs = [moments_zero(lambda e, g, sl: sx[e, :, sl])]
     moved = []
     for i, (above, below) in enumerate(rows):
-        above.wait()
-        below.wait()
+        arrived(above, below)
         start_row(RD - 1 - i, first)
         start_row(2 * RD + i, last)
         for k in range(i):
@@ -406,24 +453,26 @@
     pl.semaphore_wait(ring_sem.at[1], 3)
     send_row_to_all(me, mom_a, all_sem.at[0], all_sem.at[1])
 
-    for copy in late:
-        copy.wait()
+    arrived(*late)
     for e in range(EXT):
         ox[e] = jnp.broadcast_to(ob[e // RD, pl.ds(e % RD, 1), :], (8, NY))
         px[e] = jnp.broadcast_to(pb[e // RD, pl.ds(e % RD, 1), :], (8, NY))
-    moved[0].wait()
-    moved[1].wait()
+    arrived(moved[0], moved[1])
     powers_pair(v, 1, wu, wl, dinv, lane, 3)
-    moved[2].wait()
-    moved[3].wait()
+    arrived(moved[2], moved[3])
     powers_pair(v, 2, wu, wl, dinv, lane, 2)
     powers_pair(v, 2, wu, wl, dinv, lane, 3)
-    moved[4].wait()
-    moved[5].wait()
+    arrived(moved[4], moved[5])
 
     wait_rows(mom_a, all_sem.at[1])
     y, info = krylov_weights(unpack(jnp.sum(mom_a[...], axis=0)))
     info_ref[0] = jnp.broadcast_to(info, (CH, 128))
+
+    for copy, goes in sent:
+
+        @pl.when(goes)
+        def _():
+            copy.wait_send()
 
     def adjoint_start(e, carry):
         out = []

time: 59.8 us -> 58.8 us (0.983)
  Pallas kernels: 55.7 us -> 54.6 us
    pallas_call x1, Pallas kernels: 55.7 us -> 54.6 us  [per_device(): pl.pallas_call(step_kernel, out_shape=(jax.ShapeDtypeStruct(log_field.sha...]
where the time goes in v6:
time: 58.8 us; the launch traced here: 58.4 us
  Pallas kernels  54.6 us (93%)
  local copies, waits for them, and re-layouts  3.21 us (5%)
  between operations  0.64 us (1%)
    pallas_call x1, Pallas kernels, per_device(): pl.pallas_call(step_kernel, out_shape=(jax.ShapeDtypeStruct(log_field.sha...  54.6 us
    unnamed x2, local copies, waits for them, and re-layouts  3.21 us

profile of v6, /device:TPU:1, one launch (start us, length us, event | category | flops | bytes accessed | tf_op | source)
XLA Modules:
  0.0 58.4 jit_solution(17841485170471308295)
XLA Ops:
  0.6 54.6 %shard_map.104 = (f32[16,4,2048]{2,1,0:T(4,128)}, f32[16,256]{1,0:T(8,128)}, f32[2,16,128]{2,1,0:T(8,128)}) custom-call(f32[4,2048]{1,0:T(4,128)} %source.1, f32[4,2048]{1,0:T(4,128)} %observed.1, f32[4,2048]{1,0:T(4,128)} %precision.1, f32[4,2048]{1,0:T(4,128)} %conductivity.1, f32[16,4,2048]{2,1,0:T(4,128)} %log_field.1, f32[16,4,2048]{2,1,0:T(4,128)} %noise_field.1, ...), custom_call_target="tpu_custom_call" | custom-call | tf_op jit(solution)/shard_map/pallas_call | solution.py:615
  55.2 1.9 %copy.13 = f32[16,4,2048]{2,1,0:T(4,128)} copy(f32[16,4,2048]{2,1,0:T(4,128)} %get-tuple-element.8) | data formatting | bytes 1048576
  57.1 1.3 %copy.14 = f32[16,256]{1,0:T(8,128)} copy(f32[16,256]{1,0:T(8,128)} %get-tuple-element.9) | data formatting | bytes 32768

commit v7 on v6

--- a/solution.py
+++ b/solution.py
@@ -16,6 +16,7 @@
 EXT = 12
 TILES = NY // 128
 MESH_ID = pl.DeviceIdType.MESH
+LIMIT = 1e7
 F32 = jnp.float32
 
 
@@ -259,7 +260,7 @@
 
 def step_kernel(
     source, observed, precision, conductivity, log_field, noise_field, subspace_hbm, eigen_hbm, basis,
-    proposal, coef_ref, info_ref,
+    proposal, coef_ref, doubt_ref,
     lf, dinv, v0, v1, v2, v3, wu, wl, ws, sx, ox, px, state, cb, sb, ob, pb, mom_a, mom_b,
     nf, bm, f2, fg, ps2, got2, sum2, ps, got, sums, wide_f, pick, em, pr,
     subspace, eigen,
@@ -466,7 +467,7 @@
 
     wait_rows(mom_a, all_sem.at[1])
     y, info = krylov_weights(unpack(jnp.sum(mom_a[...], axis=0)))
-    info_ref[0] = jnp.broadcast_to(info, (CH, 128))
+    doubt = jnp.where(info < LIMIT, 0.0, 1.0)
 
     for copy, goes in sent:
 
@@ -541,7 +542,8 @@
 
     wait_rows(mom_b, all_sem.at[3])
     y, info = krylov_weights(unpack(jnp.sum(mom_b[...], axis=0)))
-    info_ref[1] = jnp.broadcast_to(info, (CH, 128))
+    doubt = doubt + jnp.where(info < LIMIT, 0.0, 1.0)
+    doubt_ref[0, 0] = jnp.sum(doubt)
 
     for r in range(RD):
         for h in range(4):
@@ -600,6 +602,81 @@
         copy.wait()
 
 
+def with_edges(value, dim):
+    down = [(i, i + 1) for i in range(N - 1)]
+    up = [(j, i) for i, j in down]
+    length = value.shape[dim]
+    before = lax.ppermute(lax.slice_in_dim(value, length - 1, length, axis=dim), AXIS, down)
+    after = lax.ppermute(lax.slice_in_dim(value, 0, 1, axis=dim), AXIS, up)
+    return jnp.concatenate([before, value, after], axis=dim)
+
+
+def apply_operator(field, weights, diagonal):
+    padded = jnp.pad(with_edges(field, 1), ((0, 0), (0, 0), (1, 1)))
+    beside = weights[0] * padded[:, :-2, 1:-1] + weights[1] * padded[:, 2:, 1:-1]
+    beside = beside + weights[2] * padded[:, 1:-1, :-2] + weights[3] * padded[:, 1:-1, 2:]
+    return diagonal * field - beside
+
+
+def chain_dot(left, right):
+    return lax.psum(jnp.sum(left * right, axis=(1, 2)), AXIS)[:, None, None]
+
+
+def solve_step_by_step(right_side, weights, diagonal):
+    scaled = right_side / diagonal
+
+    def step(_, carry):
+        solution, residual, direction, current = carry
+        applied = apply_operator(direction, weights, diagonal)
+        length = current / chain_dot(direction, applied)
+        solution = solution + length * direction
+        residual = residual - length * applied
+        scaled = residual / diagonal
+        following = chain_dot(residual, scaled)
+        return solution, residual, scaled + (following / current) * direction, following
+
+    start = (jnp.zeros_like(scaled), right_side, scaled, chain_dot(right_side, scaled))
+    return lax.fori_loop(0, ITERS, step, start)[0]
+
+
+def step_by_step(
+    source, observed, precision, conductivity, log_field, noise_field, subspace_noise, eigenvalues, basis,
+):
+    position = lax.axis_index(AXIS)
+    edges = with_edges(conductivity, 0)
+    upper = jnp.where(position == 0, conductivity[:1], edges[:1])
+    lower = jnp.where(position == N - 1, conductivity[-1:], edges[-1:])
+    padded = jnp.pad(jnp.concatenate([upper, conductivity, lower], 0), ((0, 0), (1, 1)), mode="edge")
+    weights = (
+        0.5 * (conductivity + padded[:-2, 1:-1]),
+        0.5 * (conductivity + padded[2:, 1:-1]),
+        0.5 * (conductivity + padded[1:-1, :-2]),
+        0.5 * (conductivity + padded[1:-1, 2:]),
+    )
+    reaction = jnp.exp(log_field)
+    diagonal = weights[0] + weights[1] + weights[2] + weights[3] + reaction
+
+    def solve(_, carry):
+        side, _, latest = carry
+        found = solve_step_by_step(side, weights, diagonal)
+        return precision * (found - observed), latest, found
+
+    side = jnp.broadcast_to(source, log_field.shape)
+    zeros = jnp.zeros_like(log_field)
+    _, state, adjoint = lax.fori_loop(0, 2, solve, (side, zeros, zeros))
+    gradient = -reaction * adjoint * state
+    fields = jnp.concatenate([log_field, noise_field, gradient], 0).astype(jnp.bfloat16)
+    coefs = lax.psum(jnp.einsum("cxy,rxy->cr", fields, basis, preferred_element_type=F32), AXIS)
+    state_coef, noise_coef, grad_coef = coefs[:CH], coefs[CH : 2 * CH], coefs[2 * CH :]
+    variance = 1.0 / (1.0 + eigenvalues)
+    below = 2.0 + 0.8 * variance
+    new_coef = (2.0 - 0.8 * variance) / below * state_coef - 1.6 * variance / below * grad_coef
+    new_coef = new_coef + jnp.sqrt(6.4 * variance) / below * subspace_noise
+    correction = (new_coef - 0.6 * state_coef - 0.8 * noise_coef).astype(jnp.bfloat16)
+    rebuilt = jnp.einsum("cr,rxy->cxy", correction, basis, preferred_element_type=F32)
+    return 0.6 * log_field + 0.8 * noise_field + rebuilt, new_coef
+
+
 def per_device(
     source, observed, precision, conductivity, log_field, noise_field, subspace_noise, eigenvalues, basis,
 ):
@@ -612,15 +689,15 @@
     one = pltpu.VMEM((N, 1, 128), F32)
     two = pltpu.VMEM((N, 2, 128), F32)
     half = jnp.bfloat16
-    proposal, new_coef, info = pl.pallas_call(
+    proposal, new_coef, doubt = pl.pallas_call(
         step_kernel,
         out_shape=(
             jax.ShapeDtypeStruct(log_field.shape, F32),
             jax.ShapeDtypeStruct((CH, rank), F32),
-            jax.ShapeDtypeStruct((2, CH, 128), F32),
+            jax.ShapeDtypeStruct((1, 1), F32),
         ),
         in_specs=[any_space] * 9,
-        out_specs=(any_space, vmem, vmem),
+        out_specs=(any_space, vmem, pl.BlockSpec(memory_space=pltpu.SMEM)),
         scratch_shapes=[
             wide, wide, wide, wide, wide, wide,
             pltpu.VMEM((EXT + 1, 8, NY), F32), row8, row8, row8, row8, row8, wide,
@@ -651,7 +728,14 @@
         source, observed, precision, conductivity, log_field, noise_field,
         subspace_noise, eigenvalues.reshape(1, rank), basis,
     )
-    return (proposal, new_coef)
+    return lax.cond(
+        doubt[0, 0] > 0.0,
+        lambda: step_by_step(
+            source, observed, precision, conductivity, log_field, noise_field, subspace_noise,
+            eigenvalues, basis,
+        ),
+        lambda: (proposal, new_coef),
+    )
 
 
 def solution(mesh):

time: 58.8 us -> 59.7 us (1.015)
  between operations: 0.64 us -> 1.36 us
    unnamed x2 -> x12, local copies, waits for them, and re-layouts: 3.21 us -> 3.23 us
where the time goes in v7:
time: 59.7 us; the launch traced here: 59.3 us
  Pallas kernels  54.5 us (91%)
  local copies, waits for them, and re-layouts  3.23 us (5%)
  between operations  1.36 us (2%)
    pallas_call x1, Pallas kernels, per_device(): pl.pallas_call(step_kernel, out_shape=(jax.ShapeDtypeStruct(log_field.sha...  54.5 us
    unnamed x12, local copies, waits for them, and re-layouts  3.23 us

profile of v7, /device:TPU:1, one launch (start us, length us, event | category | flops | bytes accessed | tf_op | source)
XLA Modules:
  0.0 59.3 jit_solution(7047348732762835108)
XLA Ops:
  0.6 0.0 copy-start.4
  0.6 0.0 copy-start.5
  0.7 0.0 copy-start.8
  0.7 0.0 copy-start.9
  0.7 0.0 copy-start.12
  0.7 54.5 %shard_map.108 = (f32[16,4,2048]{2,1,0:T(4,128)}, f32[16,256]{1,0:T(8,128)}, f32[1,1]{1,0:T(1,128)}) custom-call(f32[4,2048]{1,0:T(4,128)} %source.1, f32[4,2048]{1,0:T(4,128)} %observed.1, f32[4,2048]{1,0:T(4,128)} %precision.1, f32[4,2048]{1,0:T(4,128)} %conductivity.1, f32[16,4,2048]{2,1,0:T(4,128)} %log_field.1, f32[16,4,2048]{2,1,0:T(4,128)} %noise_field.1, ...), custom_call_target="tpu_custom_call" | custom-call | tf_op jit(solution)/shard_map/pallas_call | solution.py:692
  55.8 0.0 copy-done.4
  55.8 0.0 copy-done.5
  55.8 0.0 copy-done.8
  55.9 0.0 copy-done.9
  55.9 0.0 copy-done.12
  55.9 0.2 conditional.1
  56.1 1.9 %copy.82 = f32[16,4,2048]{2,1,0:T(4,128)} copy(f32[16,4,2048]{2,1,0:T(4,128)} %get-tuple-element.704) | data formatting | bytes 1048576
  58.0 1.3 %copy.83 = f32[16,256]{1,0:T(8,128)} copy(f32[16,256]{1,0:T(8,128)} %get-tuple-element.705) | data formatting | bytes 32768
Async XLA Ops:
  0.6 55.2 %copy-start.4 = (f32[4,2048]{1,0:T(4,128)S(1)}, f32[4,2048]{1,0:T(4,128)}, u32[]{:S(2)}) copy-start(f32[4,2048]{1,0:T(4,128)} %observed.1) | copy-start | bytes 98308
  0.6 55.2 %copy-start.5 = (f32[4,2048]{1,0:T(4,128)S(1)}, f32[4,2048]{1,0:T(4,128)}, u32[]{:S(2)}) copy-start(f32[4,2048]{1,0:T(4,128)} %precision.1) | copy-start | bytes 98308
  0.7 55.2 %copy-start.8 = (f32[4,2048]{1,0:T(4,128)S(1)}, f32[4,2048]{1,0:T(4,128)}, u32[]{:S(2)}) copy-start(f32[4,2048]{1,0:T(4,128)} %conductivity.1) | copy-start | bytes 98308
  0.7 55.2 %copy-start.9 = (f32[4,2048]{1,0:T(4,128)S(1)}, f32[4,2048]{1,0:T(4,128)}, u32[]{:S(2)}) copy-start(f32[4,2048]{1,0:T(4,128)} %source.1) | copy-start | bytes 98308
  0.7 55.2 %copy-start.12 = (f32[256]{0:T(256)S(1)}, f32[256]{0:T(256)}, u32[]{:S(2)}) copy-start(f32[256]{0:T(256)} %param.22) | copy-start | bytes 3076

commit v8 on v7

--- a/solution.py
+++ b/solution.py
@@ -16,7 +16,7 @@
 EXT = 12
 TILES = NY // 128
 MESH_ID = pl.DeviceIdType.MESH
-LIMIT = 1e7
+LIMIT = 2e6
 F32 = jnp.float32
 
 
@@ -117,7 +117,7 @@
     rho, pi = [one], [one]
     y = [jnp.zeros_like(one)] * ITERS
     g = m[0]
-    spread = g
+    spread, least = g, g
     gain, noise = None, None
     for step in range(ITERS):
         s = square(pi)
@@ -125,6 +125,7 @@
         size = functools.reduce(
             lambda a, b: a + b, [jnp.abs(s[l]) * (jnp.abs(m[l]) + jnp.abs(m[l + 1])) for l in range(len(s))]
         )
+        least = jnp.minimum(least, jnp.minimum(g, c))
         alpha = g / c
         part = alpha * g
         err = part * ((size / c) * (size / c) + (spread / g) * (spread / g))
@@ -150,7 +151,7 @@
         beta = following / g
         g = following
         pi = [rho[k] + beta * pi[k] if k < len(pi) else rho[k] for k in range(len(rho))]
-    return y, noise / gain
+    return y, jnp.where(least > 0.0, noise / gain, 1e30)
 
 
 def apply_row(vk, vn, wu, wl, dinv, e, lane, accs):
@@ -338,8 +339,8 @@
     for block, src, centre in ((cb, 2, 2), (sb, 1, 1)):
         early.append(remote(block.at[src], block.at[centre - 1], 1))
         early.append(remote(block.at[src], block.at[centre + 1], -1))
-    early.append(remote(cb.at[2], cb.at[0], 2))
-    early.append(remote(cb.at[2], cb.at[4], -2))
+    early.append(remote(cb.at[2, pl.ds(RD - 1, 1)], cb.at[0, pl.ds(RD - 1, 1)], 2))
+    early.append(remote(cb.at[2, pl.ds(0, 1)], cb.at[4, pl.ds(0, 1)], -2))
     rows = []
     for i in range(RD):
         rows.append(

time: 59.7 us -> 59.4 us (level)
  no operation moved by 1% of the time
where the time goes in v8:
time: 59.4 us; the launch traced here: 59.1 us
  Pallas kernels  54.3 us (91%)
  local copies, waits for them, and re-layouts  3.23 us (5%)
  between operations  1.36 us (2%)
    pallas_call x1, Pallas kernels, per_device(): pl.pallas_call(step_kernel, out_shape=(jax.ShapeDtypeStruct(log_field.sha...  54.3 us
    unnamed x12, local copies, waits for them, and re-layouts  3.23 us

profile of v8, /device:TPU:1, one launch (start us, length us, event | category | flops | bytes accessed | tf_op | source)
XLA Modules:
  0.0 59.1 jit_solution(2400266981341915041)
XLA Ops:
  0.6 0.0 copy-start.4
  0.6 0.0 copy-start.5
  0.7 0.0 copy-start.8
  0.7 0.0 copy-start.9
  0.7 0.0 copy-start.12
  0.7 54.3 %shard_map.108 = (f32[16,4,2048]{2,1,0:T(4,128)}, f32[16,256]{1,0:T(8,128)}, f32[1,1]{1,0:T(1,128)}) custom-call(f32[4,2048]{1,0:T(4,128)} %source.1, f32[4,2048]{1,0:T(4,128)} %observed.1, f32[4,2048]{1,0:T(4,128)} %precision.1, f32[4,2048]{1,0:T(4,128)} %conductivity.1, f32[16,4,2048]{2,1,0:T(4,128)} %log_field.1, f32[16,4,2048]{2,1,0:T(4,128)} %noise_field.1, ...), custom_call_target="tpu_custom_call" | custom-call | tf_op jit(solution)/shard_map/pallas_call | solution.py:693
  55.6 0.0 copy-done.4
  55.6 0.0 copy-done.5
  55.6 0.0 copy-done.8
  55.6 0.0 copy-done.9
  55.6 0.0 copy-done.12
  55.6 0.2 conditional.1
  55.9 1.9 %copy.82 = f32[16,4,2048]{2,1,0:T(4,128)} copy(f32[16,4,2048]{2,1,0:T(4,128)} %get-tuple-element.704) | data formatting | bytes 1048576
  57.7 1.3 %copy.83 = f32[16,256]{1,0:T(8,128)} copy(f32[16,256]{1,0:T(8,128)} %get-tuple-element.705) | data formatting | bytes 32768
Async XLA Ops:
  0.6 54.9 %copy-start.4 = (f32[4,2048]{1,0:T(4,128)S(1)}, f32[4,2048]{1,0:T(4,128)}, u32[]{:S(2)}) copy-start(f32[4,2048]{1,0:T(4,128)} %observed.1) | copy-start | bytes 98308
  0.6 54.9 %copy-start.5 = (f32[4,2048]{1,0:T(4,128)S(1)}, f32[4,2048]{1,0:T(4,128)}, u32[]{:S(2)}) copy-start(f32[4,2048]{1,0:T(4,128)} %precision.1) | copy-start | bytes 98308
  0.7 54.9 %copy-start.8 = (f32[4,2048]{1,0:T(4,128)S(1)}, f32[4,2048]{1,0:T(4,128)}, u32[]{:S(2)}) copy-start(f32[4,2048]{1,0:T(4,128)} %conductivity.1) | copy-start | bytes 98308
  0.7 54.9 %copy-start.9 = (f32[4,2048]{1,0:T(4,128)S(1)}, f32[4,2048]{1,0:T(4,128)}, u32[]{:S(2)}) copy-start(f32[4,2048]{1,0:T(4,128)} %source.1) | copy-start | bytes 98308
  0.7 54.9 %copy-start.12 = (f32[256]{0:T(256)S(1)}, f32[256]{0:T(256)}, u32[]{:S(2)}) copy-start(f32[256]{0:T(256)} %param.22) | copy-start | bytes 3076
